TPU v7x, 512 devices: a whole 4x4x16 slice. The times are simulated.
512 devices in a mesh: dp: 4 (over y), pipe: 32 (over z_lo, x), tensor: 4 (over z_hi, core).
Axes of the slice: x: 4, y: 4, z: 16 (z_hi: 2, z_lo: 8; z = z_hi * 8 + z_lo), core: 2. Of those that a mesh axis runs over, the one named last changes fastest.
Arguments:
- hidden: bfloat16 [1536, 2048], P(('dp', 'pipe'), 'tensor'), parts along dimension 0, may hold values from -20 to 20
- weight: bfloat16 [2048, 147456], P(None, ('pipe', 'tensor')), may hold values from -16 to 16
- targets: int32 [1536], P('dp'), parts along dimension 0, may hold values from 0 to 147455
- row_weight: float32 [1536], P('dp'), parts along dimension 0, may hold values from 2 to 20
Outputs:
- grad_hidden: bfloat16 [1536, 2048], P(('dp', 'pipe'), 'tensor'), parts along dimension 0
- row_loss: float32 [1536], P('dp'), parts along dimension 0
There are 4 independent parts, one for each index of `dp`. A program takes and returns all parts, laid end to end along the dimension named above; an argument that names none is the same for every part. Nothing has to cross between parts.
All inputs are finite; a program needn't handle non-finite values.
Results may differ from a plain program's by a relative error of at most 0.0051.
Values may be sent and summed in bfloat16 or wider, within the bound.
A program may use at most 64 MiB of HBM per device.

v0:
```python
import jax
import jax.numpy as jnp
from jax import lax
from jax.sharding import Mesh
from jax.sharding import PartitionSpec as P

TENSOR = ("tensor_0", "tensor_1")
PIPE = ("pipe_0", "pipe_1")
PIPE_TENSOR = ("pipe_0", "pipe_1", "tensor_0", "tensor_1")
DP_PIPE = ("dp", "pipe_0", "pipe_1")


def sent_to_all(x, axis):
    count = lax.axis_size(axis)
    return lax.all_to_all(jnp.broadcast_to(x[None], (count, *x.shape)), axis, 0, 0, tiled=True)


def in_order(pieces, dim):
    pieces = jnp.moveaxis(pieces, 0, dim)
    lengths = pieces.shape
    return pieces.reshape(*lengths[:dim], lengths[dim] * lengths[dim + 1], *lengths[dim + 2 :])


def gather_directly(x, axis, dim):
    pieces = sent_to_all(x, axis)
    return in_order(pieces, dim)


def collected_together(x, axis):
    leaves = jax.tree.leaves(x)
    sequence = sorted(range(len(leaves)), key=lambda k: -leaves[k].size)
    width = (1, *leaves[sequence[0]].shape)[-1]
    lines = [
        jnp.pad(leaves[k].reshape(-1), (0, -leaves[k].size % width)).reshape(-1, width)
        for k in sequence
    ]
    both, at, found = (lax.all_gather(jnp.concatenate(lines), axis), 0, {})
    for k, line in zip(sequence, lines):
        share = both[:, at : at + len(line)].reshape(len(both), -1)
        found[k] = share[:, : leaves[k].size].reshape(-1, *leaves[k].shape)
        at += len(line)
    numbers = iter(range(len(leaves)))
    return jax.tree.map(lambda _: found[next(numbers)], x)


def joined_all(x, axes, combine):
    for axis in axes:
        pieces = collected_together(x, axis)
        x = jax.tree.map(lambda part: part[0], pieces)
        for k in range(1, lax.axis_size(axis)):
            x = combine(x, jax.tree.map(lambda part: part[k], pieces))
    return x


def in_blocks(x, dim, count):
    before, after = (x.shape[:dim], x.shape[dim + 1 :])
    return jnp.moveaxis(x.reshape(*before, count, -1, *after), dim, 0)


def sent_and_summed(x, axis, dim):
    count = lax.axis_size(axis)
    pieces = lax.all_to_all(in_blocks(x, dim, count), axis, 0, 0, tiled=True)
    return jnp.sum(pieces, axis=0)


def combine_stats(earlier, later):
    top = jnp.maximum(earlier[0], later[0])
    summed = earlier[1] * jnp.exp(earlier[0] - top) + later[1] * jnp.exp(later[0] - top)
    return (top, summed, earlier[2] + later[2])


def per_device(hidden, weight, targets, row_weight):
    features = gather_directly(hidden, TENSOR, 1)
    logits = jnp.dot(gather_directly(features, PIPE, 0), weight, preferred_element_type=jnp.float32)
    vocab_dev = weight.shape[1]
    offset = (lax.axis_index(PIPE) * lax.axis_size(TENSOR) + lax.axis_index(TENSOR)) * vocab_dev
    columns = lax.broadcasted_iota(jnp.int32, logits.shape, 1) + offset
    is_target = columns == targets[:, None]
    local_label = jnp.sum(jnp.where(is_target, logits, jnp.zeros_like(logits)), axis=1)
    local_max = jnp.max(logits, axis=1)
    local_sum = jnp.sum(jnp.exp(logits - local_max[:, None]), axis=1)
    row_max, sum_exp, label_logit = joined_all(
        (local_max, local_sum, local_label), PIPE_TENSOR, combine_stats
    )
    shifted = jnp.exp(logits - row_max[:, None])
    row_loss = jnp.log(sum_exp) + row_max - label_logit
    dlogits = (
        row_weight[:, None] * (shifted / sum_exp[:, None] - is_target.astype(jnp.float32))
    ).astype(jnp.bfloat16)
    contract = (((1,), (1,)), ((), ()))
    own_rows = lax.psum_scatter(
        lax.dot_general(dlogits, weight, contract, preferred_element_type=jnp.float32),
        PIPE,
        scatter_dimension=0,
        tiled=True,
    )
    grad_hidden = sent_and_summed(own_rows, TENSOR, 1)
    return (grad_hidden.astype(jnp.bfloat16), row_loss)


def solution(mesh):
    split = Mesh(
        mesh.devices.reshape(mesh.shape["dp"], 8, 4, 2, 2),
        ("dp", "pipe_0", "pipe_1", "tensor_0", "tensor_1"),
    )
    in_specs = (P(DP_PIPE, TENSOR), P(None, PIPE_TENSOR), P("dp"), P("dp"))
    out_specs = (P(DP_PIPE, TENSOR), P("dp"))
    return jax.shard_map(
        per_device, mesh=split, in_specs=in_specs, out_specs=out_specs, check_vma=False
    )
```

profile of v0, /device:TPU:24, one launch (start us, length us, event | category | flops | bytes accessed | tf_op | source)
XLA Modules:
  0.0 397.5 jit_solution(17100249144098858912)
XLA Ops:
  0.6 0.7 broadcast_in_dim.8
  1.4 27.7 %all_to_all.15 = bf16[4,12,512]{2,1,0:T(8,128)(2,1)S(1)} all-to-all(bf16[4,12,512]{2,1,0:T(8,128)(2,1)S(1)} %broadcast_in_dim.8), channel_id=1, replica_groups=mesh['dp'=4,'pipe_0'=8,'pipe_1'=4,'tensor_0'=2,'tensor_1'=2] {'tensor_0'..., dimensions={0} | all-to-all | bytes 98304 | tf_op jit(solution)/shard_map/all_to_all | solution.py:15
  29.2 1.6 broadcast_in_dim.10
  30.8 7.9 %all-to-all-start.1 = ((bf16[32,12,2048]{2,1,0:T(8,128)(2,1)}), bf16[32,12,2048]{2,1,0:T(8,128)(2,1)S(1)}, u32[]{:S(2)}, u32[]{:S(2)}) async-start(bf16[32,12,2048]{2,1,0:T(8,128)(2,1)} %broadcast_in_dim.10), calls=%async_computation.1 | async-start | bytes 4194304 | tf_op jit(solution)/shard_map/all_to_all | solution.py:15
  38.7 95.6 %all-to-all-done.1 = bf16[32,12,2048]{2,1,0:T(8,128)(2,1)S(1)} async-done(((bf16[32,12,2048]{2,1,0:T(8,128)(2,1)}), bf16[32,12,2048]{2,1,0:T(8,128)(2,1)S(1)}, u32[]{:S(2)}, u32[]{:S(2)}) %all-to-all-start.1) | async-done | bytes 1572896 | tf_op jit(solution)/shard_map/all_to_all | solution.py:15
  134.3 1.3 reshape.917
  135.6 5.1 %fusion.63 = (f32[384]{0:T(512)S(1)}, f32[384,1152]{1,0:T(8,128)S(1)}) fusion(bf16[384,2048]{1,0:T(8,128)(2,1)} %reshape.917, bf16[2048,1152]{1,0:T(8,128)(2,1)} %param.5), kind=kOutput, calls=%fused_computation.114 | convolution fusion | flops 1812381312 | bytes 8062464 | tf_op jit(solution)/shard_map/dot_general | solution.py:74
  140.7 0.6 exponential_reduce_fusion
  141.3 46.5 %all-gather.4 = f32[8,3,384]{2,1,0:T(4,128)S(1)} all-gather(f32[1,3,384]{2,1,0:T(4,128)S(1)} %maximum_bitcast_fusion), channel_id=2, replica_groups=mesh['dp'=4,'pipe_0'=8,'pipe_1'=4,'tensor_0'=2,'tensor_1'=2] {'pipe_0'}, dimensions={0}, use_global_device_ids=true | all-gather | bytes 41472 | tf_op jit(solution)/shard_map/all_gather | solution.py:37
  187.9 12.2 %all-gather.5 = f32[4,3,384]{2,1,0:T(4,128)S(1)} all-gather(f32[1,3,384]{2,1,0:T(4,128)S(1)} %maximum_bitcast_fusion.1), channel_id=3, replica_groups=mesh['dp'=4,'pipe_0'=8,'pipe_1'=4,'tensor_0'=2,'tensor_1'=2] {'pipe_1'}, dimensions={0}, use_global_device_ids=true | all-gather | bytes 23040 | tf_op jit(solution)/shard_map/all_gather | solution.py:37
  200.2 13.1 %all-gather.6 = f32[2,3,384]{2,1,0:T(4,128)S(1)} all-gather(f32[1,3,384]{2,1,0:T(4,128)S(1)} %maximum_bitcast_fusion.2), channel_id=4, replica_groups=mesh['dp'=4,'pipe_0'=8,'pipe_1'=4,'tensor_0'=2,'tensor_1'=2] {'tensor_0'}, dimensions={0}, use_global_device_ids=true | all-gather | bytes 13824 | tf_op jit(solution)/shard_map/all_gather | solution.py:37
  213.3 1.8 all-gather.7
  215.2 0.6 add_subtract_fusion
  215.8 5.0 %fusion.5 = f32[384,2048]{1,0:T(8,128)S(1)} fusion(bf16[2048,1152]{1,0:T(8,128)(2,1)} %param.5, f32[384,1152]{1,0:T(8,128)S(1)} %get-tuple-element.19, f32[384]{0:T(512)S(1)} %get-tuple-element.10, f32[384]{0:T(512)S(1)} %get-tuple-element.11, s32[1152]{0:T(1024)S(1)} %iota_add_fusion, f32[384]{0:T(512)S(1)} %copy-done.1, s32[384]{0:T(512)S(1)} %copy-done), kind=kOutput, calls=%fused_computation.7 | convolution fusion | flops 1815035904 | bytes 9644544 | tf_op jit(solution)/shard_map/dot_general | solution.py:92
  220.8 133.7 %fusion = f32[16,2048]{1,0:T(8,128)S(1)} fusion(f32[384,2048]{1,0:T(8,128)S(1)} %fusion.5), kind=kCustom, calls=%all-reduce-scatter | all-reduce-scatter fusion | flops 1048577 | bytes 3278848
  354.5 1.3 collective-permute-start
  355.8 1.3 collective-permute-start.1
  357.2 1.3 collective-permute-start.7
  358.5 1.3 collective-permute-start.2
  359.8 1.3 collective-permute-start.3
  361.1 0.0 collective-permute-done.7
  361.1 1.3 collective-permute-start.4
  362.4 0.0 collective-permute-done
  362.4 2.5 collective-permute-start.5
  364.9 12.0 %collective-permute-start.6 = (f32[16,2048]{1,0:T(8,128)S(1)}, f32[16,2048]{1,0:T(8,128)S(1)}, u32[]{:S(2)}, u32[]{:S(2)}) collective-permute-start(f32[16,2048]{1,0:T(8,128)S(1)} %fusion), channel_id=1, source_target_pairs={{0,28},{4,32},{8,36},{12,40},{16,44},{20,48},{24,52},{28,56},{32,6... | collective-permute-start | bytes 393224
  376.9 1.3 dynamic-slice.4
  378.8 0.0 collective-permute-done.4
  378.9 0.5 collective-permute-done.6
  379.4 1.4 concatenate.16
  380.8 0.1 reshape.921
  380.9 15.9 %all_to_all.16 = f32[4,12,512]{2,1,0:T(8,128)S(1)} all-to-all(f32[4,12,512]{2,1,0:T(8,128)S(1)} %bitcast.281), channel_id=1, replica_groups=mesh['dp'=4,'pipe_0'=8,'pipe_1'=4,'tensor_0'=2,'tensor_1'=2] {'tensor_0'..., dimensions={0} | all-to-all | bytes 196608 | tf_op jit(solution)/shard_map/all_to_all | solution.py:62
  396.9 0.6 reduce_sum.29
  (29 shorter events, 0.4 us)
Async XLA Ops:
  30.8 103.5 %all-to-all-start.1 = ((bf16[32,12,2048]{2,1,0:T(8,128)(2,1)}), bf16[32,12,2048]{2,1,0:T(8,128)(2,1)S(1)}, u32[]{:S(2)}, u32[]{:S(2)}) async-start(bf16[32,12,2048]{2,1,0:T(8,128)(2,1)} %broadcast_in_dim.10), calls=%async_computation.1 | async-start | bytes 4194304 | tf_op jit(solution)/shard_map/all_to_all | solution.py:15
  135.6 5.1 %copy-start = (s32[384]{0:T(512)S(1)}, s32[384]{0:T(512)}, u32[]{:S(2)}) copy-start(s32[384]{0:T(512)} %param.6) | copy-start | bytes 4612
  140.7 75.1 %copy-start.1 = (f32[384]{0:T(512)S(1)}, f32[384]{0:T(512)}, u32[]{:S(2)}) copy-start(f32[384]{0:T(512)} %param.7) | copy-start | bytes 4612
  354.5 7.9 %collective-permute-start = (f32[16,2048]{1,0:T(8,128)S(1)}, f32[16,2048]{1,0:T(8,128)S(1)}, u32[]{:S(2)}, u32[]{:S(2)}) collective-permute-start(f32[16,2048]{1,0:T(8,128)S(1)} %fusion), channel_id=1, source_target_pairs={{0,4},{4,8},{8,12},{12,16},{16,20},{20,24},{24,28},{28,32},{32,36}... | collective-permute-start | bytes 393224
  355.8 9.1 %collective-permute-start.1 = (f32[16,2048]{1,0:T(8,128)S(1)}, f32[16,2048]{1,0:T(8,128)S(1)}, u32[]{:S(2)}, u32[]{:S(2)}) collective-permute-start(f32[16,2048]{1,0:T(8,128)S(1)} %fusion), channel_id=1, source_target_pairs={{0,8},{4,12},{8,16},{12,20},{16,24},{20,28},{24,32},{28,36},{32,40... | collective-permute-start | bytes 393224
  357.2 3.9 collective-permute-start.7
  358.5 20.3 %collective-permute-start.2 = (f32[16,2048]{1,0:T(8,128)S(1)}, f32[16,2048]{1,0:T(8,128)S(1)}, u32[]{:S(2)}, u32[]{:S(2)}) collective-permute-start(f32[16,2048]{1,0:T(8,128)S(1)} %fusion), channel_id=1, source_target_pairs={{0,12},{4,16},{8,20},{12,24},{16,28},{20,32},{24,36},{28,40},{32,4... | collective-permute-start | bytes 393224
  359.8 19.1 %collective-permute-start.3 = (f32[16,2048]{1,0:T(8,128)S(1)}, f32[16,2048]{1,0:T(8,128)S(1)}, u32[]{:S(2)}, u32[]{:S(2)}) collective-permute-start(f32[16,2048]{1,0:T(8,128)S(1)} %fusion), channel_id=1, source_target_pairs={{0,16},{4,20},{8,24},{12,28},{16,32},{20,36},{24,40},{28,44},{32,4... | collective-permute-start | bytes 393224
  361.1 17.7 %collective-permute-start.4 = (f32[16,2048]{1,0:T(8,128)S(1)}, f32[16,2048]{1,0:T(8,128)S(1)}, u32[]{:S(2)}, u32[]{:S(2)}) collective-permute-start(f32[16,2048]{1,0:T(8,128)S(1)} %fusion), channel_id=1, source_target_pairs={{0,20},{4,24},{8,28},{12,32},{16,36},{20,40},{24,44},{28,48},{32,5... | collective-permute-start | bytes 393224
  362.4 16.4 %collective-permute-start.5 = (f32[16,2048]{1,0:T(8,128)S(1)}, f32[16,2048]{1,0:T(8,128)S(1)}, u32[]{:S(2)}, u32[]{:S(2)}) collective-permute-start(f32[16,2048]{1,0:T(8,128)S(1)} %fusion), channel_id=1, source_target_pairs={{0,24},{4,28},{8,32},{12,36},{16,40},{20,44},{24,48},{28,52},{32,5... | collective-permute-start | bytes 393224
  364.9 14.5 %collective-permute-start.6 = (f32[16,2048]{1,0:T(8,128)S(1)}, f32[16,2048]{1,0:T(8,128)S(1)}, u32[]{:S(2)}, u32[]{:S(2)}) collective-permute-start(f32[16,2048]{1,0:T(8,128)S(1)} %fusion), channel_id=1, source_target_pairs={{0,28},{4,32},{8,36},{12,40},{16,44},{20,48},{24,52},{28,56},{32,6... | collective-permute-start | bytes 393224
where the time goes:
time: 401 us; the launch traced here: 397 us
  blocking collectives  251 us (63%)
  waiting for transfers between devices  96.1 us (24%)
  starting transfers between devices  30.1 us (8%)
  matrix products  10.1 us (3%)
  local copies, waits for them, and re-layouts  6.57 us (2%)
    unnamed x1, blocking collectives  134 us
    all_to_all x1, waiting for transfers between devices, sent_to_all(): lax.all_to_all(jnp.broadcast_to(x[None], (count, *x.shape)), axis, 0, 0,...  95.6 us
    all_gather x4, blocking collectives, collected_together(): both, at, found = (lax.all_gather(jnp.concatenate(lines), axis), 0, {})  73.6 us
    all_to_all x1, blocking collectives, sent_to_all(): lax.all_to_all(jnp.broadcast_to(x[None], (count, *x.shape)), axis, 0, 0,...  27.7 us
    unnamed x8, starting transfers between devices  22.2 us
    all_to_all x1, blocking collectives, sent_and_summed(): pieces = lax.all_to_all(in_blocks(x, dim, count), axis, 0, 0, tiled=True)  15.9 us
  transfers between devices with their start and end apart: 9, of which 2 were waited for; matrix products, arithmetic and copies ran while one was open for 0% of the time, Pallas kernels for 0%

commit v1 on v0

v1 whole, which is shorter than its diff:
```python
import functools

import jax
import jax.numpy as jnp
from jax import lax
from jax.experimental import pallas as pl
from jax.experimental.pallas import tpu as pltpu
from jax.sharding import Mesh
from jax.sharding import PartitionSpec as P

AXES = ("dp", "zlo", "x", "zhi", "core")
MESH = pl.DeviceIdType.MESH
F32 = jnp.float32
BF16 = jnp.bfloat16
LANES = 128
TILE = 256


def kernel(
    dims, h_ref, w_hbm, t_ref, rw_ref, out_ref, loss_ref,
    w_ref, w_sem, hid, xin, asm, x1_s, x1_r, zr_s, zr_r, zl_s, zl_r, x2_s, x2_r, cg_s, cg_r,
    logits, dlog, tcol, stat, srow, s_core, s_x, s_z, sc_s, sc_r, sx_s, sx_r, sz_s, sz_r,
    c_out, c_in, rc_s, rc_r, x_out, x_in, x_own, rx_s, rx_r, z_out, z_in, z_own, rz_s, rz_r,
    f_out, f_in, rf_s, rf_r,
):
    nzlo, nx = dims
    nz = 2 * nzlo
    rb = h_ref.shape[0]
    rows = nzlo * nx * rb
    zrows = nx * rb
    vocab = w_ref.shape[1]
    zlo, x = lax.axis_index("zlo"), lax.axis_index("x")
    zhi, core = lax.axis_index("zhi"), lax.axis_index("core")
    z = zhi * nzlo + zlo
    other = 1 - core

    def at_z(k):
        k = lax.rem(k + nz, nz)
        return {"zhi": k // nzlo, "zlo": lax.rem(k, nzlo)}

    def at_x(k):
        return {"x": lax.rem(k, nx)}

    at_core = {"core": other}

    def remote(src, dst, send, recv, where):
        return pltpu.make_async_remote_copy(
            src_ref=src, dst_ref=dst, send_sem=send, recv_sem=recv, device_id=where, device_id_type=MESH
        )

    barrier = pltpu.get_barrier_semaphore()
    near = [at_core, at_z(z + 1), at_z(z - 1)] + [at_x(x + d) for d in range(1, nx)]
    for where in near:
        pl.semaphore_signal(barrier, inc=1, device_id=where, device_id_type=MESH)
    w_copy = pltpu.make_async_copy(w_hbm, w_ref, w_sem)
    w_copy.start()

    srow[...] = jnp.zeros_like(srow)
    srow[0:1, :] = t_ref[...].astype(F32)
    srow[1:2, :] = rw_ref[...]
    tcol[...] = jnp.transpose(srow[...], (1, 0))
    pl.semaphore_wait(barrier, len(near))

    x1 = []
    for d in range(1, nx):
        q = lax.rem(x + d, nx)
        lanes = pl.ds(pl.multiple_of(q * LANES, LANES), LANES)
        x1.append(remote(h_ref.at[:, lanes], xin.at[x], x1_s.at[d - 1], x1_r.at[d - 1], at_x(q)))
        x1[-1].start()
    xin[x] = h_ref[:, pl.ds(pl.multiple_of(x * LANES, LANES), LANES)]
    for copy in x1:
        copy.wait()
    for j in range(nx):
        asm[j * rb : (j + 1) * rb, :] = xin[j].astype(F32)

    def block(k):
        k = lax.rem(k + nz, nz)
        return k // nzlo, pl.ds(pl.multiple_of(lax.rem(k, nzlo) * zrows, zrows), zrows)

    def piece(k, chunk):
        half, span = block(k)
        return hid.at[half * 2 * nx + chunk, span, :]

    mine = core * nx + x
    half_z, span_z = block(z)
    hid[half_z * 2 * nx + mine, span_z, :] = asm[...].astype(BF16)

    def right(s):
        return remote(piece(z - s, mine), piece(z - s, mine), zr_s.at[s], zr_r.at[s], at_z(z + 1))

    def left(s):
        return remote(piece(z + s, mine), piece(z + s, mine), zl_s.at[s], zl_r.at[s], at_z(z - 1))

    def over_x(k, d):
        n = lax.rem(k + nz, nz)
        return remote(piece(k, mine), piece(k, mine), x2_s.at[n, d - 1], x2_r.at[n, d - 1], at_x(x + d))

    def over_core(k):
        n = lax.rem(k + nz, nz)
        half, span = block(k)
        both = hid.at[pl.ds(half * 2 * nx + core * nx, nx), span, :]
        return remote(both, both, cg_s.at[n], cg_r.at[n], at_core)

    def start_x(k):
        for d in range(1, nx):
            over_x(k, d).start()

    def pass_to_core(k):
        for d in range(1, nx):
            over_x(k, d).wait_recv()
        over_core(k).start()

    right(0).start()
    left(0).start()
    start_x(z)
    right(0).wait_recv()

    @pl.loop(1, nz // 2)
    def _(s):
        right(s).start()
        left(s - 1).wait_recv()

        @pl.when(s < nz // 2 - 1)
        def _():
            left(s).start()

        start_x(z - s)
        start_x(z + s)
        pass_to_core(z - s + 1)

        @pl.when(s > 1)
        def _():
            pass_to_core(z + s - 1)

        right(s).wait_recv()

    start_x(z + nz // 2)
    pass_to_core(z - nz // 2 + 1)
    if nz > 2:
        pass_to_core(z + nz // 2 - 1)
    pass_to_core(z + nz // 2)
    w_copy.wait()

    @pl.loop(0, nz)
    def _(k):
        over_core(k).wait()
        for d in range(1, nx):
            over_x(k, d).wait_send()

    @pl.loop(0, nz // 2)
    def _(s):
        right(s).wait_send()

    @pl.loop(0, nz // 2 - 1)
    def _(s):
        left(s).wait_send()

    chunks = 4 * nx

    def all_rows():
        return jnp.concatenate([hid[k] for k in range(chunks)], axis=1)

    @pl.loop(0, vocab // TILE)
    def _(n):
        cols = pl.ds(pl.multiple_of(n * TILE, TILE), TILE)
        logits[:, cols] = jnp.dot(all_rows(), w_ref[:, cols], preferred_element_type=F32)

    if vocab % TILE:
        logits[:, vocab // TILE * TILE :] = jnp.dot(
            all_rows(), w_ref[:, vocab // TILE * TILE :], preferred_element_type=F32
        )

    offset = ((zlo * nx + x) * 4 + zhi * 2 + core) * vocab
    lane = lax.broadcasted_iota(jnp.int32, (zrows, LANES), 1)
    column = lax.broadcasted_iota(jnp.int32, (zrows, vocab), 1)

    def is_target(span):
        wanted = tcol[span, 0:1].astype(jnp.int32) - offset
        return column == wanted

    @pl.loop(0, nzlo)
    def _(r):
        span = pl.ds(pl.multiple_of(r * zrows, zrows), zrows)
        part = logits[span, :]
        top = jnp.max(part, axis=1, keepdims=True)
        summed = jnp.sum(jnp.exp(part - top), axis=1, keepdims=True)
        label = jnp.sum(jnp.where(is_target(span), part, 0.0), axis=1, keepdims=True)
        stat[span, :] = jnp.where(lane == 0, top, jnp.where(lane == 1, summed, jnp.where(lane == 2, label, 0.0)))

    def joined(slots):
        tops = slots[:, 0:1, :]
        top = jnp.max(tops, axis=0)
        summed = jnp.sum(slots[:, 1:2, :] * jnp.exp(tops - top[None]), axis=0)
        return top, summed, jnp.sum(slots[:, 2:3, :], axis=0)

    def put(slot, values):
        for k, value in enumerate(values):
            slot[k : k + 1, :] = value
        slot[3:4, :] = jnp.zeros_like(values[0])

    flipped = jnp.transpose(stat[...], (1, 0))
    s_core[core] = flipped[0:4, :]
    copy = remote(s_core.at[core], s_core.at[core], sc_s, sc_r, at_core)
    copy.start()
    copy.wait()
    put(s_x.at[x], joined(s_core[...]))
    copies = [
        remote(s_x.at[x], s_x.at[x], sx_s.at[d - 1], sx_r.at[d - 1], at_x(x + d)) for d in range(1, nx)
    ]
    for copy in copies:
        copy.start()
    for copy in copies:
        copy.wait()
    put(s_z.at[z], joined(s_x[...]))

    def stats_z(d):
        return remote(s_z.at[z], s_z.at[z], sz_s.at[d], sz_r.at[d], at_z(z + d))

    @pl.loop(1, nz)
    def _(d):
        stats_z(d).start()

    @pl.loop(1, nz)
    def _(d):
        stats_z(d).wait()

    top, summed, label = joined(s_z[...])
    loss_ref[...] = jnp.log(summed) + top - label
    srow[0:1, :] = top
    srow[1:2, :] = 1.0 / summed
    stat[...] = jnp.transpose(srow[...], (1, 0))

    @pl.loop(0, nzlo)
    def _(r):
        span = pl.ds(pl.multiple_of(r * zrows, zrows), zrows)
        shifted = jnp.exp(logits[span, :] - stat[span, 0:1])
        soft = shifted * stat[span, 1:2] - is_target(span).astype(F32)
        dlog[span, :] = (tcol[span, 1:2] * soft).astype(BF16)

    def product(half, who, pair):
        first = (half * 2 + who) * nx * LANES + pair * TILE
        part = w_ref[pl.ds(pl.multiple_of(first, TILE), TILE), :]
        return lax.dot_general(dlog[...], part, (((1,), (1,)), ((), ())), preferred_element_type=F32)

    pairs = nx // 2

    def to_core(n):
        two = pl.ds(2 * n, 2)
        return remote(c_out.at[two], c_in.at[two], rc_s.at[n], rc_r.at[n], at_core)

    @pl.loop(0, 2 * pairs)
    def _(n):
        part = product(n // pairs, other, lax.rem(n, pairs))
        c_out[2 * n] = part[:, :LANES].astype(BF16)
        c_out[2 * n + 1] = part[:, LANES:].astype(BF16)
        to_core(n).start()

    def to_x(half, d):
        q = lax.rem(x + d, nx)
        return remote(
            x_out.at[half * nx + q], x_in.at[half * (nx - 1) + d - 1],
            rx_s.at[half, d - 1], rx_r.at[half, d - 1], at_x(q),
        )

    @pl.loop(0, 2)
    def _(half):
        @pl.loop(0, pairs)
        def _(pair):
            n = half * pairs + pair
            part = product(half, core, pair)
            to_core(n).wait_recv()
            for k in range(2):
                whole = part[:, k * LANES : (k + 1) * LANES] + c_in[2 * n + k].astype(F32)
                x_out[2 * n + k] = whole.astype(BF16)

                @pl.when(2 * pair + k == x)
                def _():
                    x_own[half] = whole

        for d in range(1, nx):
            to_x(half, d).start()

    def to_z(half, low):
        span = pl.ds(pl.multiple_of(low * zrows, zrows), zrows)
        return remote(
            z_out.at[half, span, :], z_in.at[z], rz_s.at[half * nzlo + low], rz_r.at[z],
            {"zhi": half, "zlo": low},
        )

    @pl.loop(0, 2)
    def _(half):
        for d in range(1, nx):
            to_x(half, d).wait_recv()
        whole = x_own[half]
        for d in range(1, nx):
            whole += x_in[half * (nx - 1) + d - 1].astype(F32)
        z_out[half] = whole.astype(BF16)

        @pl.when(half == zhi)
        def _():
            z_own[...] = whole

        @pl.loop(0, nzlo)
        def _(low):
            @pl.when(half * nzlo + low != z)
            def _():
                to_z(half, low).start()

    total = z_own[span_z, :]
    asm[...] = total

    @pl.loop(0, nz)
    def _(k):
        @pl.when(k != z)
        def _():
            remote(z_in.at[k], z_in.at[k], rz_s.at[k], rz_r.at[k], at_core).wait_recv()
            asm[...] += z_in[k].astype(F32)

    for j in range(nx):
        f_out[j] = asm[j * rb : (j + 1) * rb, :].astype(BF16)
    f_in[x] = f_out[x]
    copies = [
        remote(f_out.at[lax.rem(x + d, nx)], f_in.at[x], rf_s.at[d - 1], rf_r.at[d - 1], at_x(x + d))
        for d in range(1, nx)
    ]
    for copy in copies:
        copy.start()
    for copy in copies:
        copy.wait()
    for q in range(nx):
        out_ref[:, q * LANES : (q + 1) * LANES] = f_in[q]

    @pl.loop(0, 2 * pairs)
    def _(n):
        to_core(n).wait_send()

    @pl.loop(0, 2)
    def _(half):
        for d in range(1, nx):
            to_x(half, d).wait_send()

        @pl.loop(0, nzlo)
        def _(low):
            @pl.when(half * nzlo + low != z)
            def _():
                to_z(half, low).wait_send()


def per_device(dims, hidden, weight, targets, row_weight):
    nzlo, nx = dims
    nz = 2 * nzlo
    rb, wide = hidden.shape
    depth, vocab = weight.shape
    rows = targets.shape[0]
    zrows = nx * rb
    vmem, dma = pltpu.VMEM, pltpu.SemaphoreType.DMA
    spec = pl.BlockSpec(memory_space=pltpu.VMEM)
    scratch = [
        vmem((depth, vocab), BF16), dma(()),
        vmem((4 * nx, rows, LANES), BF16), vmem((nx, rb, LANES), BF16), vmem((zrows, LANES), F32),
        dma((nx - 1,)), dma((nx - 1,)),
        dma((nz,)), dma((nz,)), dma((nz,)), dma((nz,)),
        dma((nz, nx - 1)), dma((nz, nx - 1)), dma((nz,)), dma((nz,)),
        vmem((rows, vocab), F32), vmem((rows, vocab), BF16), vmem((rows, LANES), F32),
        vmem((rows, LANES), F32), vmem((LANES, rows), F32),
        vmem((2, 4, rows), F32), vmem((nx, 4, rows), F32), vmem((nz, 4, rows), F32),
        dma(()), dma(()), dma((nx - 1,)), dma((nx - 1,)), dma((nz,)), dma((nz,)),
        vmem((2 * nx, rows, LANES), BF16), vmem((2 * nx, rows, LANES), BF16), dma((nx,)), dma((nx,)),
        vmem((2 * nx, rows, LANES), BF16), vmem((2 * (nx - 1), rows, LANES), BF16), vmem((2, rows, LANES), F32),
        dma((2, nx - 1)), dma((2, nx - 1)),
        vmem((2, rows, LANES), BF16), vmem((nz, zrows, LANES), BF16), vmem((rows, LANES), F32),
        dma((nz,)), dma((nz,)),
        vmem((nx, rb, LANES), BF16), vmem((nx, rb, LANES), BF16), dma((nx - 1,)), dma((nx - 1,)),
    ]
    grad, loss = pl.pallas_call(
        functools.partial(kernel, dims),
        out_shape=(
            jax.ShapeDtypeStruct((rb, wide), BF16),
            jax.ShapeDtypeStruct((1, rows), F32),
        ),
        in_specs=[spec, pl.BlockSpec(memory_space=pl.ANY), spec, spec],
        out_specs=(spec, spec),
        scratch_shapes=scratch,
        compiler_params=pltpu.CompilerParams(collective_id=0, has_side_effects=True),
    )(hidden, weight, targets.reshape(1, rows), row_weight.reshape(1, rows))
    return grad, loss.reshape(rows)


def on_mesh(split):
    dims = (split.shape["zlo"], split.shape["x"])
    tensor, pipe = ("zhi", "core"), ("zlo", "x")
    in_specs = (P(("dp", *pipe), tensor), P(None, (*pipe, *tensor)), P("dp"), P("dp"))
    out_specs = (P(("dp", *pipe), tensor), P("dp"))
    return jax.shard_map(
        functools.partial(per_device, dims), mesh=split, in_specs=in_specs, out_specs=out_specs, check_vma=False
    )


def solution(mesh):
    return on_mesh(Mesh(mesh.devices.reshape(mesh.shape["dp"], 8, 4, 2, 2), AXES))
```

time: 401 us -> 95 us (0.24)
  blocking collectives: 251 us -> 0 us
  waiting for transfers between devices: 96.1 us -> 0 us
  Pallas kernels: 0 us -> 89 us
  starting transfers between devices: 30.1 us -> 0 us
  matrix products: 10.1 us -> 0 us
    unnamed x1 -> x0, blocking collectives: 134 us -> none
    all_to_all x1 -> x0, waiting for transfers between devices: 95.6 us -> none  [sent_to_all(): lax.all_to_all(jnp.broadcast_to(x[None], (count, *x.shape)), axis, 0, 0,...]
    pallas_call x0 -> x1, Pallas kernels: none -> 89 us  [per_device(): pl.pallas_call(functools.partial(kernel, dims), out_shape=(jax.ShapeDtype...]
    all_gather x4 -> x0, blocking collectives: 73.6 us -> none  [collected_together(): both, at, found = (lax.all_gather(jnp.concatenate(lines), axis), 0, {})]
    all_to_all x2 -> x0, blocking collectives: 43.6 us -> none  [the longest x1 27.7 us: sent_to_all(): lax.all_to_all(jnp.broadcast_to(x[None], (count, *x.shape)), axis, 0, 0,...]
    unnamed x8 -> x0, starting transfers between devices: 22.2 us -> none
    dot_general x2 -> x0, matrix products: 10.1 us -> none  [the longest x1 5.11 us: per_device(): jnp.dot(gather_directly(features, PIPE, 0), weight, preferred_element_typ...]
    all_to_all x1 -> x0, starting transfers between devices: 7.87 us -> none  [sent_to_all(): lax.all_to_all(jnp.broadcast_to(x[None], (count, *x.shape)), axis, 0, 0,...]
  transfers between devices with their start and end apart: 9 -> 0, of which waited for: 2 -> 0; matrix products, arithmetic and copies ran while one was open for 0% -> 0% of each run, Pallas kernels for 0% -> 0%
where the time goes in v1:
time: 95 us; the launch traced here: 94.7 us
  Pallas kernels  89 us (94%)
  local copies, waits for them, and re-layouts  3.81 us (4%)
  other arithmetic  1.27 us (1%)
    pallas_call x1, Pallas kernels, per_device(): pl.pallas_call(functools.partial(kernel, dims), out_shape=(jax.ShapeDtype...  89 us

profile of v1, /device:TPU:24, one launch (start us, length us, event | category | flops | bytes accessed | tf_op | source)
XLA Modules:
  0.0 94.7 jit_solution(15711582829943057078)
XLA Ops:
  0.6 1.2 %reshape.13.t_ref = s32[1,384]{1,0:T(1,128)} reshape(s32[384]{0:T(512)} %param.6) | data formatting | bytes 3072 | tf_op jit(solution)/shard_map/reshape | solution.py:385
  1.9 1.2 %reshape.14.rw_ref = f32[1,384]{1,0:T(1,128)} reshape(f32[384]{0:T(512)} %param.7) | data formatting | bytes 3072 | tf_op jit(solution)/shard_map/reshape | solution.py:385
  3.1 89.0 %shard_map.59 = (bf16[12,512]{1,0:T(8,128)(2,1)}, f32[1,384]{1,0:T(1,128)}) custom-call(bf16[12,512]{1,0:T(8,128)(2,1)} %h_ref.1, bf16[2048,1152]{1,0:T(8,128)(2,1)} %w_hbm.1, s32[1,384]{1,0:T(1,128)} %reshape.13.t_ref, f32[1,384]{1,0:T(1,128)} %reshape.14.rw_ref), custom_call_target="tpu_custom_call" | custom-call | tf_op jit(solution)/shard_map/pallas_call | solution.py:375
  92.1 1.3 %reduce = f32[384]{0:T(512)} reduce(f32[1,384]{1,0:T(1,128)} %get-tuple-element.5, f32[]{:T(128)} %constant.1), dimensions={0}, to_apply=%get-tuple-element.5.reduce_sub_computation | reduce | bytes 3076 | tf_op jit(solution)/shard_map/pallas_call | solution.py:375
  93.4 1.3 %copy.7 = bf16[12,512]{1,0:T(8,128)(2,1)} copy(bf16[12,512]{1,0:T(8,128)(2,1)} %get-tuple-element.8) | data formatting | bytes 24576

commit v2 on v0

v2 whole, which is shorter than its diff:
```python
import functools

import jax
import jax.numpy as jnp
from jax import lax
from jax.experimental import pallas as pl
from jax.experimental.pallas import tpu as pltpu
from jax.sharding import Mesh
from jax.sharding import PartitionSpec as P

AXES = ("dp", "zlo", "x", "zhi", "core")
MESH = pl.DeviceIdType.MESH
F32 = jnp.float32
BF16 = jnp.bfloat16
LANES = 128
TILE = 256


def kernel(
    dims, h_ref, w_hbm, t_ref, rw_ref, out_ref, loss_ref,
    w_ref, w_sem, hid, pieces, tall, wide_rows, zg_s, zg_r, xg_s, xg_r, cg_s, cg_r,
    logits, soft, tcol, stat, srow, s_core, s_x, s_z, sc_s, sc_r, sx_s, sx_r, sz_s, sz_r,
    t_out, t_in, t_own, tx_in, tc_s, tc_r, tx_s, tx_r,
    c_out, c_in, rc_s, rc_r, whole_ref, x_out, x_in, x_own, rx_s, rx_r,
    acc, z_out, z_in, rz_s, rz_r,
):
    nzlo, nx = dims
    nz = 2 * nzlo
    rb, wide = h_ref.shape
    quarters = wide // LANES
    rows = nzlo * nx * rb
    xrows = nzlo * rb
    step = 48
    vocab = w_ref.shape[1]
    zlo, x = lax.axis_index("zlo"), lax.axis_index("x")
    zhi, core = lax.axis_index("zhi"), lax.axis_index("core")
    z = zhi * nzlo + zlo
    other = 1 - core
    pairs = wide // TILE

    def at_z(k):
        k = lax.rem(k + nz, nz)
        return {"zhi": k // nzlo, "zlo": lax.rem(k, nzlo)}

    def at_x(k):
        return {"x": lax.rem(k, nx)}

    at_core = {"core": other}

    def remote(src, dst, send, recv, where):
        return pltpu.make_async_remote_copy(
            src_ref=src, dst_ref=dst, send_sem=send, recv_sem=recv, device_id=where, device_id_type=MESH
        )

    def rows_of(k, size):
        return pl.ds(pl.multiple_of(k * size, size), size)

    barrier = pltpu.get_barrier_semaphore()
    partners = [at_z(z + d) for d in range(1, nz)] + [at_x(x + d) for d in range(1, nx)] + [at_core]
    for where in partners:
        pl.semaphore_signal(barrier, inc=1, device_id=where, device_id_type=MESH)
    w_copy = pltpu.make_async_copy(w_hbm, w_ref, w_sem)
    w_copy.start()

    srow[...] = jnp.zeros_like(srow)
    srow[0:1, :] = t_ref[...].astype(F32).reshape(1, rows)
    srow[1:2, :] = rw_ref[...].reshape(1, rows)
    stat[...] = jnp.transpose(srow[...], (1, 0))
    for i in range(nx):
        for j in range(nzlo):
            to, of = (i * nzlo + j) * rb, (j * nx + i) * rb
            tcol[to : to + rb, :] = stat[of : of + rb, :]

    for j in range(quarters):
        tall[0, j * rb : (j + 1) * rb, :] = h_ref[:, j * LANES : (j + 1) * LANES].astype(F32)
    pieces[z] = tall[0].astype(BF16)

    offset = ((zlo * nx + x) * 4 + zhi * 2 + core) * vocab
    lane = lax.broadcasted_iota(jnp.int32, (step, LANES), 1)
    column = lax.broadcasted_iota(jnp.int32, (step, vocab), 1)

    def is_target(span):
        wanted = tcol[span, 0:1].astype(jnp.int32) - offset
        return column == wanted

    @pl.loop(0, rows // step)
    def _(r):
        span = rows_of(r, step)
        soft[span, :] = jnp.where(is_target(span), 1.0, 0.0).astype(BF16)

    def product(half, who, pair):
        first = (half * 2 + who) * wide + pair * TILE
        part = w_ref[pl.ds(pl.multiple_of(first, TILE), TILE), :]
        return lax.dot_general(soft[...], part, (((1,), (1,)), ((), ())), preferred_element_type=F32)

    def tile(pair):
        return rows_of(pair, TILE)

    w_copy.wait()

    @pl.loop(0, 2 * pairs)
    def _(n):
        half, pair = n // pairs, lax.rem(n, pairs)
        t_out[half, :, tile(pair)] = product(half, other, pair).astype(BF16)
        t_own[half, :, tile(pair)] = product(half, core, pair).astype(BF16)

    pl.semaphore_wait(barrier, len(partners))

    def gather_z(d):
        k = lax.rem(z + d + nz, nz)
        return remote(pieces.at[z], pieces.at[z], zg_s.at[k], zg_r.at[z], at_z(z + d))

    for d in range(1, nz // 2):
        gather_z(d).start()
        gather_z(-d).start()
    gather_z(nz // 2).start()

    def t_core(half):
        return remote(t_out.at[half], t_in.at[half], tc_s.at[half], tc_r.at[half], at_core)

    t_core(0).start()
    t_core(1).start()

    size = min(4, nzlo)
    groups = nz // size
    grows = size * rb
    per_half = groups // 2

    def place(g, chunk_x):
        first = chunk_x * xrows + lax.rem(g, per_half) * grows
        return hid.at[(g // per_half) * 2 + core, pl.ds(pl.multiple_of(first, grows), grows), :]

    def over_x(g, d):
        return remote(place(g, x), place(g, x), xg_s.at[g, d - 1], xg_r.at[g, d - 1], at_x(x + d))

    def over_core(g, d):
        whose = lax.rem(x + d, nx)
        return remote(place(g, whose), place(g, whose), cg_s.at[g, d], cg_r.at[g, d], at_core)

    def pass_to_core(g):
        for d in range(1, nx):
            over_x(g, nx - d).wait_recv()
            over_core(g, d).start()

    def take_group(g):
        for i in range(size):
            k = g * size + i

            @pl.when(k != z)
            def _():
                remote(pieces.at[k], pieces.at[k], zg_s.at[k], zg_r.at[k], at_core).wait_recv()

            tall[i] = pieces[k].astype(F32)
            for j in range(quarters):
                wide_rows[i * rb : (i + 1) * rb, j * LANES : (j + 1) * LANES] = tall[i, j * rb : (j + 1) * rb, :]
        first = x * xrows + lax.rem(g, per_half) * grows
        hid[(g // per_half) * 2 + core, pl.ds(pl.multiple_of(first, grows), grows), :] = wide_rows[...].astype(BF16)
        for d in range(1, nx):
            over_x(g, d).start()
        over_core(g, 0).start()

    def in_turn(i):
        if groups == 2:
            return lax.rem(z // size + i, groups)
        shift = jnp.where(i == 2, 3, jnp.where(i == 3, 2, i))
        return lax.rem(z // size + shift, groups)

    @pl.loop(0, groups)
    def _(i):
        take_group(in_turn(i))

        @pl.when(i > 0)
        def _():
            pass_to_core(in_turn(i - 1))

    def t_over_x(half, d):
        q = lax.rem(x + d, nx)
        return remote(
            t_own.at[half, rows_of(q, xrows), :], tx_in.at[d - 1, half], tx_s.at[half, d - 1], tx_r.at[half, d - 1], at_x(q)
        )

    for half in range(2):
        t_core(half).wait_recv()

        @pl.loop(0, rows // step)
        def _(r):
            span = rows_of(r, step)
            t_own[half, span, :] = (t_own[half, span, :].astype(F32) + t_in[half, span, :].astype(F32)).astype(BF16)

    pass_to_core(in_turn(groups - 1))

    for half in range(2):
        for d in range(1, nx):
            t_over_x(half, d).start()

    @pl.loop(0, groups)
    def _(g):
        for d in range(nx):
            over_core(g, d).wait_recv()

    def all_rows():
        return jnp.concatenate([hid[k] for k in range(4)], axis=1)

    @pl.loop(0, vocab // TILE)
    def _(n):
        cols = tile(n)
        logits[:, cols] = jnp.dot(all_rows(), w_ref[:, cols], preferred_element_type=F32)

    if vocab % TILE:
        logits[:, vocab // TILE * TILE :] = jnp.dot(
            all_rows(), w_ref[:, vocab // TILE * TILE :], preferred_element_type=F32
        )

    @pl.loop(0, rows // step)
    def _(r):
        span = rows_of(r, step)
        part = logits[span, :]
        top = jnp.max(part, axis=1, keepdims=True)
        shifted = jnp.exp(part - top)
        soft[span, :] = shifted.astype(BF16)
        summed = jnp.sum(shifted, axis=1, keepdims=True)
        label = jnp.sum(jnp.where(is_target(span), part, 0.0), axis=1, keepdims=True)
        stat[span, :] = jnp.where(lane == 0, top, jnp.where(lane == 1, summed, jnp.where(lane == 2, label, 0.0)))

    def joined(slots):
        tops = slots[:, 0:1, :]
        top = jnp.max(tops, axis=0)
        summed = jnp.sum(slots[:, 1:2, :] * jnp.exp(tops - top[None]), axis=0)
        return top, summed, jnp.sum(slots[:, 2:3, :], axis=0)

    def put(slot, values):
        for k, value in enumerate(values):
            slot[k : k + 1, :] = value
        slot[3:4, :] = jnp.zeros_like(values[0])

    flipped = jnp.transpose(stat[...], (1, 0))
    s_core[core] = flipped[0:4, :]
    stats_core = remote(s_core.at[core], s_core.at[core], sc_s, sc_r, at_core)
    stats_core.start()

    def to_core(half, pair):
        n = half * pairs + pair
        part = c_out.at[half, :, tile(pair)]
        return remote(part, c_in.at[half, :, tile(pair)], rc_s.at[n], rc_r.at[n], at_core)

    def for_partner(half):
        @pl.loop(0, pairs)
        def _(pair):
            c_out[half, :, tile(pair)] = product(half, other, pair).astype(BF16)
            to_core(half, pair).start()

    for_partner(0)
    stats_core.wait()
    put(s_x.at[x], joined(s_core[...]))
    stats_x = [
        remote(s_x.at[x], s_x.at[x], sx_s.at[d - 1], sx_r.at[d - 1], at_x(x + d)) for d in range(1, nx)
    ]
    for copy in stats_x:
        copy.start()
    core_top = s_x[x, 0:1, :]
    srow[0:1, :] = jnp.exp(s_core[core, 0:1, :] - core_top)
    srow[1:2, :] = jnp.exp(s_core[other, 0:1, :] - core_top)
    stat[...] = jnp.transpose(srow[...], (1, 0))
    for_partner(1)

    def to_x(half, pair, d):
        q = lax.rem(x + d, nx)
        n = half * pairs + pair
        return remote(
            x_out.at[half, rows_of(q, xrows), tile(pair)], x_in.at[d - 1, half, :, tile(pair)],
            rx_s.at[n, d - 1], rx_r.at[n, d - 1], at_x(q),
        )

    @pl.loop(0, 2 * pairs)
    def _(n):
        half, pair = n // pairs, lax.rem(n, pairs)
        whole_ref[...] = product(half, core, pair)
        to_core(half, pair).wait_recv()

        @pl.loop(0, rows // step)
        def _(r):
            span = rows_of(r, step)
            got = c_in[half, span, tile(pair)].astype(F32)
            whole = whole_ref[span, :] * stat[span, 0:1] + got * stat[span, 1:2]
            whole_ref[span, :] = whole
            x_out[half, span, tile(pair)] = whole.astype(BF16)

        x_own[half, :, tile(pair)] = whole_ref[rows_of(x, xrows), :]
        for d in range(1, nx):
            to_x(half, pair, d).start()

    for copy in stats_x:
        copy.wait()
    put(s_z.at[z], joined(s_x[...]))

    def stats_z(d):
        return remote(s_z.at[z], s_z.at[z], sz_s.at[d], sz_r.at[d], at_z(z + d))

    @pl.loop(1, nz)
    def _(d):
        stats_z(d).start()

    x_top = s_z[z, 0:1, :]
    srow[0:1, :] = jnp.exp(s_x[x, 0:1, :] - x_top)
    for d in range(1, nx):
        srow[d : d + 1, :] = jnp.exp(s_x[lax.rem(x + nx - d, nx), 0:1, :] - x_top)
    stat[...] = jnp.transpose(srow[...], (1, 0))
    own_rows = rows_of(x, xrows)

    @pl.loop(0, 2)
    def _(half):
        for d in range(1, nx):
            for pair in range(pairs):
                to_x(half, pair, d).wait_recv()
        whole = x_own[half] * stat[own_rows, 0:1]
        for d in range(1, nx):
            whole += x_in[d - 1, half].astype(F32) * stat[own_rows, d : d + 1]
        acc[half] = whole

    @pl.loop(1, nz)
    def _(d):
        stats_z(d).wait()

    top, summed, label = joined(s_z[...])
    srow[0:1, :] = jnp.exp(x_top - top) / summed
    srow[1:2, :] = jnp.log(summed) + top - label
    stat[...] = jnp.transpose(srow[...], (1, 0))

    def to_z(k):
        return remote(z_out.at[k], z_in.at[z], rz_s.at[k], rz_r.at[z], at_z(k))

    @pl.loop(0, 2)
    def _(half):
        weight = tcol[own_rows, 1:2]
        hit = t_own[half, own_rows, :].astype(F32)
        for d in range(1, nx):
            t_over_x(half, d).wait_recv()
            hit += tx_in[d - 1, half].astype(F32)
        acc[half] = acc[half] * (weight * stat[own_rows, 0:1]) - weight * hit
        for low in range(nzlo):
            slot = low % 4
            for j in range(quarters):
                tall[slot, j * rb : (j + 1) * rb, :] = acc[half, low * rb : (low + 1) * rb, j * LANES : (j + 1) * LANES]
            k = half * nzlo + low

            @pl.when(k == z)
            def _():
                tall[4] = tall[slot]

            @pl.when(k != z)
            def _():
                z_out[k] = tall[slot].astype(BF16)
                to_z(k).start()

    for i in range(nx):
        for j in range(nzlo):
            of, to = (i * nzlo + j) * rb, (j * nx + i) * rb
            logits[to : to + rb, 0:LANES] = stat[of : of + rb, :]
    loss_ref[...] = jnp.transpose(logits[:, 0:LANES], (1, 0))[1:2, :].reshape(rows)

    @pl.loop(0, nz)
    def _(k):
        @pl.when(k != z)
        def _():
            remote(z_in.at[k], z_in.at[k], rz_s.at[k], rz_r.at[k], at_core).wait_recv()
            tall[4] += z_in[k].astype(F32)

    for j in range(quarters):
        out_ref[:, j * LANES : (j + 1) * LANES] = tall[4, j * rb : (j + 1) * rb, :].astype(BF16)

    @pl.loop(1, nz)
    def _(d):
        gather_z(d).wait_send()
        to_z(lax.rem(z + d, nz)).wait_send()

    @pl.loop(0, groups)
    def _(g):
        over_core(g, 0).wait_send()
        for d in range(1, nx):
            over_core(g, d).wait_send()
            over_x(g, d).wait_send()

    @pl.loop(0, 2)
    def _(half):
        t_core(half).wait_send()
        for d in range(1, nx):
            t_over_x(half, d).wait_send()
        for pair in range(pairs):
            to_core(half, pair).wait_send()
            for d in range(1, nx):
                to_x(half, pair, d).wait_send()


def per_device(dims, hidden, weight, targets, row_weight):
    nzlo, nx = dims
    nz = 2 * nzlo
    rb, wide = hidden.shape
    depth, vocab = weight.shape
    rows = targets.shape[0]
    xrows = nzlo * rb
    size = min(4, nzlo)
    groups = nz // size
    tallness = rb * wide // LANES
    pairs = wide // TILE
    vmem, dma = pltpu.VMEM, pltpu.SemaphoreType.DMA
    spec = pl.BlockSpec(memory_space=pltpu.VMEM)
    halves = vmem((2, rows, wide), BF16)
    scratch = [
        vmem((depth, vocab), BF16), dma(()),
        vmem((4, rows, wide), BF16), vmem((nz, tallness, LANES), BF16), vmem((5, tallness, LANES), F32),
        vmem((size * rb, wide), F32),
        dma((nz,)), dma((nz,)), dma((groups, nx - 1)), dma((groups, nx - 1)), dma((groups, nx)), dma((groups, nx)),
        vmem((rows, vocab), F32), vmem((rows, vocab), BF16), vmem((rows, LANES), F32),
        vmem((rows, LANES), F32), vmem((LANES, rows), F32),
        vmem((2, 4, rows), F32), vmem((nx, 4, rows), F32), vmem((nz, 4, rows), F32),
        dma(()), dma(()), dma((nx - 1,)), dma((nx - 1,)), dma((nz,)), dma((nz,)),
        halves, halves, halves, vmem((nx - 1, 2, xrows, wide), BF16),
        dma((2,)), dma((2,)), dma((2, nx - 1)), dma((2, nx - 1)),
        halves, halves, dma((2 * pairs,)), dma((2 * pairs,)), vmem((rows, TILE), F32),
        halves, vmem((nx - 1, 2, xrows, wide), BF16), vmem((2, xrows, wide), F32),
        dma((2 * pairs, nx - 1)), dma((2 * pairs, nx - 1)),
        vmem((2, xrows, wide), F32), vmem((nz, tallness, LANES), BF16), vmem((nz, tallness, LANES), BF16),
        dma((nz,)), dma((nz,)),
    ]
    return pl.pallas_call(
        functools.partial(kernel, dims),
        out_shape=(
            jax.ShapeDtypeStruct((rb, wide), BF16),
            jax.ShapeDtypeStruct((rows,), F32),
        ),
        in_specs=[spec, pl.BlockSpec(memory_space=pl.ANY), spec, spec],
        out_specs=(spec, spec),
        scratch_shapes=scratch,
        compiler_params=pltpu.CompilerParams(collective_id=0, has_side_effects=True),
    )(hidden, weight, targets, row_weight)


def on_mesh(split):
    dims = (split.shape["zlo"], split.shape["x"])
    tensor, pipe = ("zhi", "core"), ("zlo", "x")
    in_specs = (P(("dp", *pipe), tensor), P(None, (*pipe, *tensor)), P("dp"), P("dp"))
    out_specs = (P(("dp", *pipe), tensor), P("dp"))
    return jax.shard_map(
        functools.partial(per_device, dims), mesh=split, in_specs=in_specs, out_specs=out_specs, check_vma=False
    )


def solution(mesh):
    return on_mesh(Mesh(mesh.devices.reshape(mesh.shape["dp"], 8, 4, 2, 2), AXES))
```

time: 401 us -> 74.6 us (0.19)
  blocking collectives: 251 us -> 0 us
  waiting for transfers between devices: 96.1 us -> 0 us
  Pallas kernels: 0 us -> 71 us
  starting transfers between devices: 30.1 us -> 0 us
  matrix products: 10.1 us -> 0 us
  local copies, waits for them, and re-layouts: 6.57 us -> 2.55 us
    unnamed x1 -> x0, blocking collectives: 134 us -> none
    all_to_all x1 -> x0, waiting for transfers between devices: 95.6 us -> none  [sent_to_all(): lax.all_to_all(jnp.broadcast_to(x[None], (count, *x.shape)), axis, 0, 0,...]
    all_gather x4 -> x0, blocking collectives: 73.6 us -> none  [collected_together(): both, at, found = (lax.all_gather(jnp.concatenate(lines), axis), 0, {})]
    pallas_call x0 -> x1, Pallas kernels: none -> 71 us  [per_device(): pl.pallas_call(functools.partial(kernel, dims), out_shape=(jax.ShapeDtype...]
    all_to_all x2 -> x0, blocking collectives: 43.6 us -> none  [the longest x1 27.7 us: sent_to_all(): lax.all_to_all(jnp.broadcast_to(x[None], (count, *x.shape)), axis, 0, 0,...]
    unnamed x8 -> x0, starting transfers between devices: 22.2 us -> none
    dot_general x2 -> x0, matrix products: 10.1 us -> none  [the longest x1 5.11 us: per_device(): jnp.dot(gather_directly(features, PIPE, 0), weight, preferred_element_typ...]
    all_to_all x1 -> x0, starting transfers between devices: 7.87 us -> none  [sent_to_all(): lax.all_to_all(jnp.broadcast_to(x[None], (count, *x.shape)), axis, 0, 0,...]
  transfers between devices with their start and end apart: 9 -> 0, of which waited for: 2 -> 0; matrix products, arithmetic and copies ran while one was open for 0% -> 0% of each run, Pallas kernels for 0% -> 0%
where the time goes in v2:
time: 74.6 us; the launch traced here: 74.2 us
  Pallas kernels  71 us (95%)
  local copies, waits for them, and re-layouts  2.55 us (3%)
    pallas_call x1, Pallas kernels, per_device(): pl.pallas_call(functools.partial(kernel, dims), out_shape=(jax.ShapeDtype...  71 us
    unnamed x2, local copies, waits for them, and re-layouts  2.55 us

profile of v2, /device:TPU:24, one launch (start us, length us, event | category | flops | bytes accessed | tf_op | source)
XLA Modules:
  0.0 74.2 jit_solution(7572286076455157240)
XLA Ops:
  0.6 71.0 %shard_map.59 = (bf16[12,512]{1,0:T(8,128)(2,1)}, f32[384]{0:T(512)}) custom-call(bf16[12,512]{1,0:T(8,128)(2,1)} %h_ref.1, bf16[2048,1152]{1,0:T(8,128)(2,1)} %w_hbm.1, s32[384]{0:T(512)} %t_ref.1, f32[384]{0:T(512)} %rw_ref.1), custom_call_target="tpu_custom_call" | custom-call | tf_op jit(solution)/shard_map/pallas_call | solution.py:425
  71.7 1.3 %copy.8 = bf16[12,512]{1,0:T(8,128)(2,1)} copy(bf16[12,512]{1,0:T(8,128)(2,1)} %get-tuple-element.4) | data formatting | bytes 24576
  73.0 1.2 %copy.9 = f32[384]{0:T(512)} copy(f32[384]{0:T(512)} %get-tuple-element.5) | data formatting | bytes 3072

commit v3 on v2

--- a/solution.py
+++ b/solution.py
@@ -17,12 +17,12 @@
 
 
 def kernel(
-    dims, h_ref, w_hbm, t_ref, rw_ref, out_ref, loss_ref,
-    w_ref, w_sem, hid, pieces, tall, wide_rows, zg_s, zg_r, xg_s, xg_r, cg_s, cg_r,
-    logits, soft, tcol, stat, srow, s_core, s_x, s_z, sc_s, sc_r, sx_s, sx_r, sz_s, sz_r,
+    dims, h_hbm, w_hbm, t_hbm, rw_hbm, out_ref, loss_ref,
+    h_ref, t_ref, rw_ref, in_sem, w_ref, w_sem, hid, pieces, tall, wide_rows, zg_s, zg_r, xg_s, xg_r, cg_s, cg_r,
+    logits, soft, tcol, stat, srow, s_cx, s_z, s_loss, sc_s, sc_r, sz_s, sz_r, sl_s, sl_r,
     t_out, t_in, t_own, tx_in, tc_s, tc_r, tx_s, tx_r,
     c_out, c_in, rc_s, rc_r, whole_ref, x_out, x_in, x_own, rx_s, rx_r,
-    acc, z_out, z_in, rz_s, rz_r,
+    acc, z_out, z_in, rz_s, rz_r, flat,
 ):
     nzlo, nx = dims
     nz = 2 * nzlo
@@ -32,6 +32,7 @@
     xrows = nzlo * rb
     step = 48
     vocab = w_ref.shape[1]
+    per_x = xrows // step
     zlo, x = lax.axis_index("zlo"), lax.axis_index("x")
     zhi, core = lax.axis_index("zhi"), lax.axis_index("core")
     z = zhi * nzlo + zlo
@@ -59,12 +60,21 @@
     partners = [at_z(z + d) for d in range(1, nz)] + [at_x(x + d) for d in range(1, nx)] + [at_core]
     for where in partners:
         pl.semaphore_signal(barrier, inc=1, device_id=where, device_id_type=MESH)
+    small = [
+        pltpu.make_async_copy(t_hbm, t_ref, in_sem.at[0]),
+        pltpu.make_async_copy(rw_hbm, rw_ref, in_sem.at[1]),
+        pltpu.make_async_copy(h_hbm, h_ref, in_sem.at[2]),
+    ]
+    for copy in small:
+        copy.start()
     w_copy = pltpu.make_async_copy(w_hbm, w_ref, w_sem)
     w_copy.start()
 
     srow[...] = jnp.zeros_like(srow)
-    srow[0:1, :] = t_ref[...].astype(F32).reshape(1, rows)
-    srow[1:2, :] = rw_ref[...].reshape(1, rows)
+    for copy in small:
+        copy.wait()
+    srow[0:1, 0:rows] = t_ref[...].astype(F32).reshape(1, rows)
+    srow[1:2, 0:rows] = rw_ref[...].reshape(1, rows)
     stat[...] = jnp.transpose(srow[...], (1, 0))
     for i in range(nx):
         for j in range(nzlo):
@@ -96,6 +106,21 @@
     def tile(pair):
         return rows_of(pair, TILE)
 
+    def padded(r):
+        first = (r // per_x) * LANES + lax.rem(r, per_x) * step
+        return pl.ds(pl.multiple_of(first, 16), step)
+
+    pl.semaphore_wait(barrier, len(partners))
+
+    def gather_z(d):
+        k = lax.rem(z + d + nz, nz)
+        return remote(pieces.at[z], pieces.at[z], zg_s.at[k], zg_r.at[z], at_z(z + d))
+
+    for d in range(1, nz // 2):
+        gather_z(d).start()
+        gather_z(-d).start()
+    gather_z(nz // 2).start()
+
     w_copy.wait()
 
     @pl.loop(0, 2 * pairs)
@@ -103,17 +128,6 @@
         half, pair = n // pairs, lax.rem(n, pairs)
         t_out[half, :, tile(pair)] = product(half, other, pair).astype(BF16)
         t_own[half, :, tile(pair)] = product(half, core, pair).astype(BF16)
-
-    pl.semaphore_wait(barrier, len(partners))
-
-    def gather_z(d):
-        k = lax.rem(z + d + nz, nz)
-        return remote(pieces.at[z], pieces.at[z], zg_s.at[k], zg_r.at[z], at_z(z + d))
-
-    for d in range(1, nz // 2):
-        gather_z(d).start()
-        gather_z(-d).start()
-    gather_z(nz // 2).start()
 
     def t_core(half):
         return remote(t_out.at[half], t_in.at[half], tc_s.at[half], tc_r.at[half], at_core)
@@ -220,7 +234,7 @@
         soft[span, :] = shifted.astype(BF16)
         summed = jnp.sum(shifted, axis=1, keepdims=True)
         label = jnp.sum(jnp.where(is_target(span), part, 0.0), axis=1, keepdims=True)
-        stat[span, :] = jnp.where(lane == 0, top, jnp.where(lane == 1, summed, jnp.where(lane == 2, label, 0.0)))
+        stat[padded(r), :] = jnp.where(lane == 0, top, jnp.where(lane == 1, summed, jnp.where(lane == 2, label, 0.0)))
 
     def joined(slots):
         tops = slots[:, 0:1, :]
@@ -228,15 +242,18 @@
         summed = jnp.sum(slots[:, 1:2, :] * jnp.exp(tops - top[None]), axis=0)
         return top, summed, jnp.sum(slots[:, 2:3, :], axis=0)
 
-    def put(slot, values):
-        for k, value in enumerate(values):
-            slot[k : k + 1, :] = value
-        slot[3:4, :] = jnp.zeros_like(values[0])
-
     flipped = jnp.transpose(stat[...], (1, 0))
-    s_core[core] = flipped[0:4, :]
-    stats_core = remote(s_core.at[core], s_core.at[core], sc_s, sc_r, at_core)
-    stats_core.start()
+    here = x * 2 + core
+    s_cx[here] = flipped[0:4, :]
+
+    def stats_cx(n):
+        d, c = n // 2, n % 2
+        return remote(
+            s_cx.at[here], s_cx.at[here], sc_s.at[n], sc_r.at[n], {"x": lax.rem(x + d, nx), "core": lax.rem(core + c, 2)}
+        )
+
+    for n in range(1, 2 * nx):
+        stats_cx(n).start()
 
     def to_core(half, pair):
         n = half * pairs + pair
@@ -250,18 +267,13 @@
             to_core(half, pair).start()
 
     for_partner(0)
-    stats_core.wait()
-    put(s_x.at[x], joined(s_core[...]))
-    stats_x = [
-        remote(s_x.at[x], s_x.at[x], sx_s.at[d - 1], sx_r.at[d - 1], at_x(x + d)) for d in range(1, nx)
-    ]
-    for copy in stats_x:
-        copy.start()
-    core_top = s_x[x, 0:1, :]
-    srow[0:1, :] = jnp.exp(s_core[core, 0:1, :] - core_top)
-    srow[1:2, :] = jnp.exp(s_core[other, 0:1, :] - core_top)
+    stats_cx(1).wait()
+    mine = s_cx[here, 0:1, :]
+    theirs = s_cx[x * 2 + other, 0:1, :]
+    core_top = jnp.maximum(mine, theirs)
+    srow[0:1, :] = jnp.exp(mine - core_top)
+    srow[1:2, :] = jnp.exp(theirs - core_top)
     stat[...] = jnp.transpose(srow[...], (1, 0))
-    for_partner(1)
 
     def to_x(half, pair, d):
         q = lax.rem(x + d, nx)
@@ -271,9 +283,7 @@
             rx_s.at[n, d - 1], rx_r.at[n, d - 1], at_x(q),
         )
 
-    @pl.loop(0, 2 * pairs)
-    def _(n):
-        half, pair = n // pairs, lax.rem(n, pairs)
+    def for_self(half, pair):
         whole_ref[...] = product(half, core, pair)
         to_core(half, pair).wait_recv()
 
@@ -281,7 +291,7 @@
         def _(r):
             span = rows_of(r, step)
             got = c_in[half, span, tile(pair)].astype(F32)
-            whole = whole_ref[span, :] * stat[span, 0:1] + got * stat[span, 1:2]
+            whole = whole_ref[span, :] * stat[padded(r), 0:1] + got * stat[padded(r), 1:2]
             whole_ref[span, :] = whole
             x_out[half, span, tile(pair)] = whole.astype(BF16)
 
@@ -289,9 +299,28 @@
         for d in range(1, nx):
             to_x(half, pair, d).start()
 
-    for copy in stats_x:
-        copy.wait()
-    put(s_z.at[z], joined(s_x[...]))
+    @pl.loop(0, pairs)
+    def _(pair):
+        for_self(0, pair)
+
+    for_partner(1)
+
+    @pl.loop(0, pairs)
+    def _(pair):
+        for_self(1, pair)
+
+    for n in range(2, 2 * nx):
+        stats_cx(n).wait()
+    all_top, all_sum, all_label = joined(s_cx[...])
+    srow[0:1, :] = all_top
+    srow[1:2, :] = all_sum
+    srow[2:3, :] = all_label
+    for d in range(nx):
+        there = lax.rem(x + nx - d, nx) * 2
+        top = jnp.maximum(s_cx[there, 0:1, :], s_cx[there + 1, 0:1, :])
+        srow[4 + d : 5 + d, :] = jnp.exp(top - all_top)
+    own_lanes = pl.ds(pl.multiple_of(x * LANES, LANES), LANES)
+    s_z[z] = srow[0:4, own_lanes]
 
     def stats_z(d):
         return remote(s_z.at[z], s_z.at[z], sz_s.at[d], sz_r.at[d], at_z(z + d))
@@ -300,11 +329,7 @@
     def _(d):
         stats_z(d).start()
 
-    x_top = s_z[z, 0:1, :]
-    srow[0:1, :] = jnp.exp(s_x[x, 0:1, :] - x_top)
-    for d in range(1, nx):
-        srow[d : d + 1, :] = jnp.exp(s_x[lax.rem(x + nx - d, nx), 0:1, :] - x_top)
-    stat[...] = jnp.transpose(srow[...], (1, 0))
+    flat[...] = jnp.transpose(srow[:, own_lanes], (1, 0))
     own_rows = rows_of(x, xrows)
 
     @pl.loop(0, 2)
@@ -312,9 +337,9 @@
         for d in range(1, nx):
             for pair in range(pairs):
                 to_x(half, pair, d).wait_recv()
-        whole = x_own[half] * stat[own_rows, 0:1]
-        for d in range(1, nx):
-            whole += x_in[d - 1, half].astype(F32) * stat[own_rows, d : d + 1]
+        whole = x_own[half] * flat[0:xrows, 4:5]
+        for d in range(1, nx):
+            whole += x_in[d - 1, half].astype(F32) * flat[0:xrows, 4 + d : 5 + d]
         acc[half] = whole
 
     @pl.loop(1, nz)
@@ -322,9 +347,12 @@
         stats_z(d).wait()
 
     top, summed, label = joined(s_z[...])
-    srow[0:1, :] = jnp.exp(x_top - top) / summed
-    srow[1:2, :] = jnp.log(summed) + top - label
-    stat[...] = jnp.transpose(srow[...], (1, 0))
+    srow[0:1, 0:LANES] = jnp.exp(s_z[z, 0:1, :] - top) / summed
+    flat[...] = jnp.transpose(srow[:, 0:LANES], (1, 0))
+    s_loss[x] = jnp.broadcast_to(jnp.log(summed) + top - label, (8, LANES))
+
+    def losses(d):
+        return remote(s_loss.at[x], s_loss.at[x], sl_s.at[d - 1], sl_r.at[d - 1], at_x(x + d))
 
     def to_z(k):
         return remote(z_out.at[k], z_in.at[z], rz_s.at[k], rz_r.at[z], at_z(k))
@@ -336,7 +364,7 @@
         for d in range(1, nx):
             t_over_x(half, d).wait_recv()
             hit += tx_in[d - 1, half].astype(F32)
-        acc[half] = acc[half] * (weight * stat[own_rows, 0:1]) - weight * hit
+        acc[half] = acc[half] * (weight * flat[0:xrows, 0:1]) - weight * hit
         for low in range(nzlo):
             slot = low % 4
             for j in range(quarters):
@@ -352,11 +380,18 @@
                 z_out[k] = tall[slot].astype(BF16)
                 to_z(k).start()
 
+    for d in range(1, nx):
+        losses(d).start()
+    for d in range(1, nx):
+        losses(d).wait()
+    for i in range(nx):
+        srow[0:1, i * LANES : (i + 1) * LANES] = s_loss[i, 0:1, :]
+    stat[...] = jnp.transpose(srow[...], (1, 0))
     for i in range(nx):
         for j in range(nzlo):
-            of, to = (i * nzlo + j) * rb, (j * nx + i) * rb
+            of, to = i * LANES + j * rb, (j * nx + i) * rb
             logits[to : to + rb, 0:LANES] = stat[of : of + rb, :]
-    loss_ref[...] = jnp.transpose(logits[:, 0:LANES], (1, 0))[1:2, :].reshape(rows)
+    loss_ref[...] = jnp.transpose(logits[:, 0:LANES], (1, 0))[0:1, :].reshape(rows)
 
     @pl.loop(0, nz)
     def _(k):
@@ -406,21 +441,22 @@
     spec = pl.BlockSpec(memory_space=pltpu.VMEM)
     halves = vmem((2, rows, wide), BF16)
     scratch = [
+        vmem((rb, wide), BF16), vmem((rows,), jnp.int32), vmem((rows,), F32), dma((3,)),
         vmem((depth, vocab), BF16), dma(()),
         vmem((4, rows, wide), BF16), vmem((nz, tallness, LANES), BF16), vmem((5, tallness, LANES), F32),
         vmem((size * rb, wide), F32),
         dma((nz,)), dma((nz,)), dma((groups, nx - 1)), dma((groups, nx - 1)), dma((groups, nx)), dma((groups, nx)),
         vmem((rows, vocab), F32), vmem((rows, vocab), BF16), vmem((rows, LANES), F32),
-        vmem((rows, LANES), F32), vmem((LANES, rows), F32),
-        vmem((2, 4, rows), F32), vmem((nx, 4, rows), F32), vmem((nz, 4, rows), F32),
-        dma(()), dma(()), dma((nx - 1,)), dma((nx - 1,)), dma((nz,)), dma((nz,)),
+        vmem((nx * LANES, LANES), F32), vmem((LANES, nx * LANES), F32),
+        vmem((2 * nx, 4, nx * LANES), F32), vmem((nz, 4, LANES), F32), vmem((nx, 8, LANES), F32),
+        dma((2 * nx,)), dma((2 * nx,)), dma((nz,)), dma((nz,)), dma((nx - 1,)), dma((nx - 1,)),
         halves, halves, halves, vmem((nx - 1, 2, xrows, wide), BF16),
         dma((2,)), dma((2,)), dma((2, nx - 1)), dma((2, nx - 1)),
         halves, halves, dma((2 * pairs,)), dma((2 * pairs,)), vmem((rows, TILE), F32),
         halves, vmem((nx - 1, 2, xrows, wide), BF16), vmem((2, xrows, wide), F32),
         dma((2 * pairs, nx - 1)), dma((2 * pairs, nx - 1)),
         vmem((2, xrows, wide), F32), vmem((nz, tallness, LANES), BF16), vmem((nz, tallness, LANES), BF16),
-        dma((nz,)), dma((nz,)),
+        dma((nz,)), dma((nz,)), vmem((LANES, LANES), F32),
     ]
     return pl.pallas_call(
         functools.partial(kernel, dims),
@@ -428,7 +464,7 @@
             jax.ShapeDtypeStruct((rb, wide), BF16),
             jax.ShapeDtypeStruct((rows,), F32),
         ),
-        in_specs=[spec, pl.BlockSpec(memory_space=pl.ANY), spec, spec],
+        in_specs=[pl.BlockSpec(memory_space=pl.ANY)] * 4,
         out_specs=(spec, spec),
         scratch_shapes=scratch,
         compiler_params=pltpu.CompilerParams(collective_id=0, has_side_effects=True),

time: 74.6 us -> 72.5 us (0.972)
  Pallas kernels: 71 us -> 68.4 us
    pallas_call x1, Pallas kernels: 71 us -> 68.4 us  [per_device(): pl.pallas_call(functools.partial(kernel, dims), out_shape=(jax.ShapeDtype...]
where the time goes in v3:
time: 72.5 us; the launch traced here: 71.6 us
  Pallas kernels  68.4 us (94%)
  local copies, waits for them, and re-layouts  2.55 us (4%)
    pallas_call x1, Pallas kernels, per_device(): pl.pallas_call(functools.partial(kernel, dims), out_shape=(jax.ShapeDtype...  68.4 us
    unnamed x2, local copies, waits for them, and re-layouts  2.55 us

profile of v3, /device:TPU:24, one launch (start us, length us, event | category | flops | bytes accessed | tf_op | source)
XLA Modules:
  0.0 71.6 jit_solution(17460407453837255705)
XLA Ops:
  0.6 68.4 %shard_map.59 = (bf16[12,512]{1,0:T(8,128)(2,1)}, f32[384]{0:T(512)}) custom-call(bf16[12,512]{1,0:T(8,128)(2,1)} %h_hbm.1, bf16[2048,1152]{1,0:T(8,128)(2,1)} %w_hbm.1, s32[384]{0:T(512)} %t_hbm.1, f32[384]{0:T(512)} %rw_hbm.1), custom_call_target="tpu_custom_call" | custom-call | tf_op jit(solution)/shard_map/pallas_call | solution.py:461
  69.1 1.3 %copy.8 = bf16[12,512]{1,0:T(8,128)(2,1)} copy(bf16[12,512]{1,0:T(8,128)(2,1)} %get-tuple-element.4) | data formatting | bytes 24576
  70.4 1.2 %copy.9 = f32[384]{0:T(512)} copy(f32[384]{0:T(512)} %get-tuple-element.5) | data formatting | bytes 3072

commit v4 on v3

--- a/solution.py
+++ b/solution.py
@@ -22,7 +22,7 @@
     logits, soft, tcol, stat, srow, s_cx, s_z, s_loss, sc_s, sc_r, sz_s, sz_r, sl_s, sl_r,
     t_out, t_in, t_own, tx_in, tc_s, tc_r, tx_s, tx_r,
     c_out, c_in, rc_s, rc_r, whole_ref, x_out, x_in, x_own, rx_s, rx_r,
-    acc, z_out, z_in, rz_s, rz_r, flat,
+    acc, z_out, z_in, rz_s, rz_r, flat, factor,
 ):
     nzlo, nx = dims
     nz = 2 * nzlo
@@ -57,7 +57,8 @@
         return pl.ds(pl.multiple_of(k * size, size), size)
 
     barrier = pltpu.get_barrier_semaphore()
-    partners = [at_z(z + d) for d in range(1, nz)] + [at_x(x + d) for d in range(1, nx)] + [at_core]
+    reach = nz // 4
+    partners = [at_z(z + d) for d in range(-reach, reach + 1) if d] + [at_x(x + d) for d in range(1, nx)] + [at_core]
     for where in partners:
         pl.semaphore_signal(barrier, inc=1, device_id=where, device_id_type=MESH)
     small = [
@@ -112,14 +113,15 @@
 
     pl.semaphore_wait(barrier, len(partners))
 
-    def gather_z(d):
-        k = lax.rem(z + d + nz, nz)
-        return remote(pieces.at[z], pieces.at[z], zg_s.at[k], zg_r.at[z], at_z(z + d))
-
-    for d in range(1, nz // 2):
-        gather_z(d).start()
-        gather_z(-d).start()
-    gather_z(nz // 2).start()
+    def gather_z(whose, d, n):
+        k = lax.rem(whose + nz, nz)
+        return remote(pieces.at[k], pieces.at[k], zg_s.at[n], zg_r.at[k], at_z(z + d))
+
+    direct = [gather_z(z, sign * d, 2 * (reach - d) + (sign > 0)) for d in range(reach, 0, -1) for sign in (-1, 1)]
+    onward = [gather_z(z - reach, d, 2 * reach + d - 1) for d in range(reach - 1, 0, -1)]
+    backward = [gather_z(z + reach, -d, 3 * reach + d - 2) for d in range(reach, 0, -1)]
+    for copy in direct:
+        copy.start()
 
     w_copy.wait()
 
@@ -160,9 +162,11 @@
         for i in range(size):
             k = g * size + i
 
-            @pl.when(k != z)
+            away = lax.rem(k - z + nz, nz)
+
+            @pl.when((away != 0) & (away != reach) & (away != nz - reach))
             def _():
-                remote(pieces.at[k], pieces.at[k], zg_s.at[k], zg_r.at[k], at_core).wait_recv()
+                remote(pieces.at[k], pieces.at[k], zg_s.at[0], zg_r.at[k], at_core).wait_recv()
 
             tall[i] = pieces[k].astype(F32)
             for j in range(quarters):
@@ -174,10 +178,14 @@
         over_core(g, 0).start()
 
     def in_turn(i):
-        if groups == 2:
-            return lax.rem(z // size + i, groups)
-        shift = jnp.where(i == 2, 3, jnp.where(i == 3, 2, i))
-        return lax.rem(z // size + shift, groups)
+        half = lax.rem(zhi + i // per_half, 2)
+        return half * per_half + lax.rem(zlo // size + i, per_half)
+
+    for source, copies in ((z - reach, onward), (z + reach, backward)):
+        k = lax.rem(source + nz, nz)
+        remote(pieces.at[k], pieces.at[k], zg_s.at[0], zg_r.at[k], at_core).wait_recv()
+        for copy in copies:
+            copy.start()
 
     @pl.loop(0, groups)
     def _(i):
@@ -201,29 +209,45 @@
             span = rows_of(r, step)
             t_own[half, span, :] = (t_own[half, span, :].astype(F32) + t_in[half, span, :].astype(F32)).astype(BF16)
 
-    pass_to_core(in_turn(groups - 1))
-
-    for half in range(2):
-        for d in range(1, nx):
-            t_over_x(half, d).start()
-
-    @pl.loop(0, groups)
-    def _(g):
-        for d in range(nx):
-            over_core(g, d).wait_recv()
-
-    def all_rows():
-        return jnp.concatenate([hid[k] for k in range(4)], axis=1)
+    def arrived(half):
+        @pl.loop(0, per_half)
+        def _(g):
+            for d in range(nx):
+                over_core(half * per_half + g, d).wait_recv()
+
+    def half_rows(half):
+        return jnp.concatenate([hid[2 * half], hid[2 * half + 1]], axis=1)
+
+    def depth(half):
+        return pl.ds(pl.multiple_of(half * 2 * wide, 2 * wide), 2 * wide)
+
+    last = vocab // TILE * TILE
+    arrived(zhi)
 
     @pl.loop(0, vocab // TILE)
     def _(n):
         cols = tile(n)
-        logits[:, cols] = jnp.dot(all_rows(), w_ref[:, cols], preferred_element_type=F32)
+        logits[:, cols] = jnp.dot(half_rows(zhi), w_ref[depth(zhi), cols], preferred_element_type=F32)
 
     if vocab % TILE:
-        logits[:, vocab // TILE * TILE :] = jnp.dot(
-            all_rows(), w_ref[:, vocab // TILE * TILE :], preferred_element_type=F32
-        )
+        logits[:, last:] = jnp.dot(half_rows(zhi), w_ref[depth(zhi), last:], preferred_element_type=F32)
+
+    pass_to_core(in_turn(groups - 1))
+
+    for half in range(2):
+        for d in range(1, nx):
+            t_over_x(half, d).start()
+
+    far = 1 - zhi
+    arrived(far)
+
+    @pl.loop(0, vocab // TILE)
+    def _(n):
+        cols = tile(n)
+        logits[:, cols] += jnp.dot(half_rows(far), w_ref[depth(far), cols], preferred_element_type=F32)
+
+    if vocab % TILE:
+        logits[:, last:] += jnp.dot(half_rows(far), w_ref[depth(far), last:], preferred_element_type=F32)
 
     @pl.loop(0, rows // step)
     def _(r):
@@ -271,9 +295,11 @@
     mine = s_cx[here, 0:1, :]
     theirs = s_cx[x * 2 + other, 0:1, :]
     core_top = jnp.maximum(mine, theirs)
-    srow[0:1, :] = jnp.exp(mine - core_top)
-    srow[1:2, :] = jnp.exp(theirs - core_top)
-    stat[...] = jnp.transpose(srow[...], (1, 0))
+    for k, own in enumerate((mine, theirs)):
+        srow[...] = jnp.broadcast_to(jnp.exp(own - core_top), srow.shape)
+        stat[...] = jnp.transpose(srow[...], (1, 0))
+        for i in range(nx):
+            factor[k, i * xrows : (i + 1) * xrows, :] = stat[i * LANES : i * LANES + xrows, :]
 
     def to_x(half, pair, d):
         q = lax.rem(x + d, nx)
@@ -287,13 +313,11 @@
         whole_ref[...] = product(half, core, pair)
         to_core(half, pair).wait_recv()
 
-        @pl.loop(0, rows // step)
-        def _(r):
-            span = rows_of(r, step)
-            got = c_in[half, span, tile(pair)].astype(F32)
-            whole = whole_ref[span, :] * stat[padded(r), 0:1] + got * stat[padded(r), 1:2]
-            whole_ref[span, :] = whole
-            x_out[half, span, tile(pair)] = whole.astype(BF16)
+        for k in range(TILE // LANES):
+            lanes = pl.ds(pl.multiple_of(pair * TILE + k * LANES, LANES), LANES)
+            whole = whole_ref[:, k * LANES : (k + 1) * LANES] * factor[0] + c_in[half, :, lanes].astype(F32) * factor[1]
+            whole_ref[:, k * LANES : (k + 1) * LANES] = whole
+            x_out[half, :, lanes] = whole.astype(BF16)
 
         x_own[half, :, tile(pair)] = whole_ref[rows_of(x, xrows), :]
         for d in range(1, nx):
@@ -304,10 +328,6 @@
         for_self(0, pair)
 
     for_partner(1)
-
-    @pl.loop(0, pairs)
-    def _(pair):
-        for_self(1, pair)
 
     for n in range(2, 2 * nx):
         stats_cx(n).wait()
@@ -332,6 +352,10 @@
     flat[...] = jnp.transpose(srow[:, own_lanes], (1, 0))
     own_rows = rows_of(x, xrows)
 
+    @pl.loop(0, pairs)
+    def _(pair):
+        for_self(1, pair)
+
     @pl.loop(0, 2)
     def _(half):
         for d in range(1, nx):
@@ -375,10 +399,12 @@
             def _():
                 tall[4] = tall[slot]
 
-            @pl.when(k != z)
-            def _():
-                z_out[k] = tall[slot].astype(BF16)
-                to_z(k).start()
+            z_out[k] = tall[slot].astype(BF16)
+
+    to_z(lax.rem(z + nz // 2, nz)).start()
+    for d in range(nz // 2 - 1, 0, -1):
+        to_z(lax.rem(z + d, nz)).start()
+        to_z(lax.rem(z + nz - d, nz)).start()
 
     for d in range(1, nx):
         losses(d).start()
@@ -405,8 +431,10 @@
 
     @pl.loop(1, nz)
     def _(d):
-        gather_z(d).wait_send()
         to_z(lax.rem(z + d, nz)).wait_send()
+
+    for copy in direct + onward + backward:
+        copy.wait_send()
 
     @pl.loop(0, groups)
     def _(g):
@@ -456,7 +484,7 @@
         halves, vmem((nx - 1, 2, xrows, wide), BF16), vmem((2, xrows, wide), F32),
         dma((2 * pairs, nx - 1)), dma((2 * pairs, nx - 1)),
         vmem((2, xrows, wide), F32), vmem((nz, tallness, LANES), BF16), vmem((nz, tallness, LANES), BF16),
-        dma((nz,)), dma((nz,)), vmem((LANES, LANES), F32),
+        dma((nz,)), dma((nz,)), vmem((LANES, LANES), F32), vmem((2, rows, LANES), F32),
     ]
     return pl.pallas_call(
         functools.partial(kernel, dims),

time: 72.5 us -> 68.2 us (0.941)
  Pallas kernels: 68.4 us -> 64.6 us
    pallas_call x1, Pallas kernels: 68.4 us -> 64.6 us  [per_device(): pl.pallas_call(functools.partial(kernel, dims), out_shape=(jax.ShapeDtype...]
where the time goes in v4:
time: 68.2 us; the launch traced here: 67.8 us
  Pallas kernels  64.6 us (95%)
  local copies, waits for them, and re-layouts  2.55 us (4%)
    pallas_call x1, Pallas kernels, per_device(): pl.pallas_call(functools.partial(kernel, dims), out_shape=(jax.ShapeDtype...  64.6 us
    unnamed x2, local copies, waits for them, and re-layouts  2.55 us

profile of v4, /device:TPU:24, one launch (start us, length us, event | category | flops | bytes accessed | tf_op | source)
XLA Modules:
  0.0 67.8 jit_solution(5641913749251642877)
XLA Ops:
  0.6 64.6 %shard_map.59 = (bf16[12,512]{1,0:T(8,128)(2,1)}, f32[384]{0:T(512)}) custom-call(bf16[12,512]{1,0:T(8,128)(2,1)} %h_hbm.1, bf16[2048,1152]{1,0:T(8,128)(2,1)} %w_hbm.1, s32[384]{0:T(512)} %t_hbm.1, f32[384]{0:T(512)} %rw_hbm.1), custom_call_target="tpu_custom_call" | custom-call | tf_op jit(solution)/shard_map/pallas_call | solution.py:489
  65.3 1.3 %copy.8 = bf16[12,512]{1,0:T(8,128)(2,1)} copy(bf16[12,512]{1,0:T(8,128)(2,1)} %get-tuple-element.4) | data formatting | bytes 24576
  66.6 1.2 %copy.9 = f32[384]{0:T(512)} copy(f32[384]{0:T(512)} %get-tuple-element.5) | data formatting | bytes 3072

commit v5 on v4

--- a/solution.py
+++ b/solution.py
@@ -187,20 +187,14 @@
         for copy in copies:
             copy.start()
 
-    @pl.loop(0, groups)
-    def _(i):
-        take_group(in_turn(i))
-
-        @pl.when(i > 0)
-        def _():
-            pass_to_core(in_turn(i - 1))
-
     def t_over_x(half, d):
         q = lax.rem(x + d, nx)
         return remote(
             t_own.at[half, rows_of(q, xrows), :], tx_in.at[d - 1, half], tx_s.at[half, d - 1], tx_r.at[half, d - 1], at_x(q)
         )
 
+    for i in range(groups):
+        take_group(in_turn(i))
     for half in range(2):
         t_core(half).wait_recv()
 
@@ -208,6 +202,9 @@
         def _(r):
             span = rows_of(r, step)
             t_own[half, span, :] = (t_own[half, span, :].astype(F32) + t_in[half, span, :].astype(F32)).astype(BF16)
+
+    for i in range(per_half):
+        pass_to_core(in_turn(i))
 
     def arrived(half):
         @pl.loop(0, per_half)
@@ -232,7 +229,8 @@
     if vocab % TILE:
         logits[:, last:] = jnp.dot(half_rows(zhi), w_ref[depth(zhi), last:], preferred_element_type=F32)
 
-    pass_to_core(in_turn(groups - 1))
+    for i in range(per_half, groups):
+        pass_to_core(in_turn(i))
 
     for half in range(2):
         for d in range(1, nx):
@@ -489,8 +487,8 @@
     return pl.pallas_call(
         functools.partial(kernel, dims),
         out_shape=(
-            jax.ShapeDtypeStruct((rb, wide), BF16),
-            jax.ShapeDtypeStruct((rows,), F32),
+            pltpu.VMEM((rb, wide), BF16),
+            pltpu.VMEM((rows,), F32),
         ),
         in_specs=[pl.BlockSpec(memory_space=pl.ANY)] * 4,
         out_specs=(spec, spec),

time: 68.2 us -> 65.1 us (0.955)
  Pallas kernels: 64.6 us -> 63.1 us
  local copies, waits for them, and re-layouts: 2.55 us -> 1.19 us
    pallas_call x1, Pallas kernels: 64.6 us -> 63.1 us  [per_device(): pl.pallas_call(functools.partial(kernel, dims), out_shape=(pltpu.VMEM((rb...]
    unnamed x2, local copies, waits for them, and re-layouts: 2.55 us -> 1.19 us
where the time goes in v5:
time: 65.1 us; the launch traced here: 64.9 us
  Pallas kernels  63.1 us (97%)
  local copies, waits for them, and re-layouts  1.19 us (2%)
    pallas_call x1, Pallas kernels, per_device(): pl.pallas_call(functools.partial(kernel, dims), out_shape=(pltpu.VMEM((rb...  63.1 us

profile of v5, /device:TPU:24, one launch (start us, length us, event | category | flops | bytes accessed | tf_op | source)
XLA Modules:
  0.0 64.9 jit_solution(8436424992155635926)
XLA Ops:
  0.6 63.1 %shard_map.59 = (bf16[12,512]{1,0:T(8,128)(2,1)S(1)}, f32[384]{0:T(512)S(1)}) custom-call(bf16[12,512]{1,0:T(8,128)(2,1)} %h_hbm.1, bf16[2048,1152]{1,0:T(8,128)(2,1)} %w_hbm.1, s32[384]{0:T(512)} %t_hbm.1, f32[384]{0:T(512)} %rw_hbm.1), custom_call_target="tpu_custom_call" | custom-call | tf_op jit(solution)/shard_map/pallas_call | solution.py:487
  63.7 0.6 copy.8
  64.3 0.6 copy.9

commit v6 on v5

--- a/solution.py
+++ b/solution.py
@@ -20,9 +20,9 @@
     dims, h_hbm, w_hbm, t_hbm, rw_hbm, out_ref, loss_ref,
     h_ref, t_ref, rw_ref, in_sem, w_ref, w_sem, hid, pieces, tall, wide_rows, zg_s, zg_r, xg_s, xg_r, cg_s, cg_r,
     logits, soft, tcol, stat, srow, s_cx, s_z, s_loss, sc_s, sc_r, sz_s, sz_r, sl_s, sl_r,
-    t_out, t_in, t_own, tx_in, tc_s, tc_r, tx_s, tx_r,
-    c_out, c_in, rc_s, rc_r, whole_ref, x_out, x_in, x_own, rx_s, rx_r,
-    acc, z_out, z_in, rz_s, rz_r, flat, factor,
+    t_out, t_in, t_own, tc_s, tc_r, to_in, tm_in, tm_out, to_s, to_r, tm_s, tm_r, t_rows, tx_in, tx_s, tx_r,
+    c_out, c_in, rc_s, rc_r, whole_ref, x_out, x_in, x_own, rx_s, rx_r, t_wide,
+    acc, z_out, z_in, rz_s, rz_r, flat, factor, own_col, tall_col,
 ):
     nzlo, nx = dims
     nz = 2 * nzlo
@@ -62,18 +62,35 @@
     for where in partners:
         pl.semaphore_signal(barrier, inc=1, device_id=where, device_id_type=MESH)
     small = [
+        pltpu.make_async_copy(h_hbm, h_ref, in_sem.at[2]),
         pltpu.make_async_copy(t_hbm, t_ref, in_sem.at[0]),
         pltpu.make_async_copy(rw_hbm, rw_ref, in_sem.at[1]),
-        pltpu.make_async_copy(h_hbm, h_ref, in_sem.at[2]),
     ]
     for copy in small:
         copy.start()
     w_copy = pltpu.make_async_copy(w_hbm, w_ref, w_sem)
     w_copy.start()
 
+    small[0].wait()
+    for j in range(quarters):
+        tall[0, j * rb : (j + 1) * rb, :] = h_ref[:, j * LANES : (j + 1) * LANES].astype(F32)
+    pieces[z] = tall[0].astype(BF16)
+
+    pl.semaphore_wait(barrier, len(partners))
+
+    def gather_z(whose, d, n):
+        k = lax.rem(whose + nz, nz)
+        return remote(pieces.at[k], pieces.at[k], zg_s.at[n], zg_r.at[k], at_z(z + d))
+
+    direct = [gather_z(z, sign * d, 2 * (reach - d) + (sign > 0)) for d in range(reach, 0, -1) for sign in (-1, 1)]
+    onward = [gather_z(z - reach, d, 2 * reach + d - 1) for d in range(reach - 1, 0, -1)]
+    backward = [gather_z(z + reach, -d, 3 * reach + d - 2) for d in range(reach, 0, -1)]
+    for copy in direct:
+        copy.start()
+
     srow[...] = jnp.zeros_like(srow)
-    for copy in small:
-        copy.wait()
+    small[1].wait()
+    small[2].wait()
     srow[0:1, 0:rows] = t_ref[...].astype(F32).reshape(1, rows)
     srow[1:2, 0:rows] = rw_ref[...].reshape(1, rows)
     stat[...] = jnp.transpose(srow[...], (1, 0))
@@ -81,23 +98,21 @@
         for j in range(nzlo):
             to, of = (i * nzlo + j) * rb, (j * nx + i) * rb
             tcol[to : to + rb, :] = stat[of : of + rb, :]
-
-    for j in range(quarters):
-        tall[0, j * rb : (j + 1) * rb, :] = h_ref[:, j * LANES : (j + 1) * LANES].astype(F32)
-    pieces[z] = tall[0].astype(BF16)
+    own_rows = rows_of(x, xrows)
+    own_col[...] = tcol[own_rows, :]
 
     offset = ((zlo * nx + x) * 4 + zhi * 2 + core) * vocab
     lane = lax.broadcasted_iota(jnp.int32, (step, LANES), 1)
     column = lax.broadcasted_iota(jnp.int32, (step, vocab), 1)
 
-    def is_target(span):
-        wanted = tcol[span, 0:1].astype(jnp.int32) - offset
+    def is_target(span, of=tcol):
+        wanted = of[span, 0:1].astype(jnp.int32) - offset
         return column == wanted
 
     @pl.loop(0, rows // step)
     def _(r):
         span = rows_of(r, step)
-        soft[span, :] = jnp.where(is_target(span), 1.0, 0.0).astype(BF16)
+        soft[span, :] = jnp.where(is_target(span, stat), 1.0, 0.0).astype(BF16)
 
     def product(half, who, pair):
         first = (half * 2 + who) * wide + pair * TILE
@@ -110,18 +125,6 @@
     def padded(r):
         first = (r // per_x) * LANES + lax.rem(r, per_x) * step
         return pl.ds(pl.multiple_of(first, 16), step)
-
-    pl.semaphore_wait(barrier, len(partners))
-
-    def gather_z(whose, d, n):
-        k = lax.rem(whose + nz, nz)
-        return remote(pieces.at[k], pieces.at[k], zg_s.at[n], zg_r.at[k], at_z(z + d))
-
-    direct = [gather_z(z, sign * d, 2 * (reach - d) + (sign > 0)) for d in range(reach, 0, -1) for sign in (-1, 1)]
-    onward = [gather_z(z - reach, d, 2 * reach + d - 1) for d in range(reach - 1, 0, -1)]
-    backward = [gather_z(z + reach, -d, 3 * reach + d - 2) for d in range(reach, 0, -1)]
-    for copy in direct:
-        copy.start()
 
     w_copy.wait()
 
@@ -187,11 +190,43 @@
         for copy in copies:
             copy.start()
 
-    def t_over_x(half, d):
+    span_z = nz // 2
+
+    def t_block(k):
+        k = lax.rem(k + nz, nz)
+        return t_own.at[k // nzlo, rows_of(lax.rem(k, nzlo), nx * rb), :]
+
+    def t_odd(sign, j):
+        i = (sign + 1) // 2
+        return remote(t_block(z + sign * (2 * j + 1)), to_in.at[i, j], to_s.at[i, j], to_r.at[i, j], at_z(z + sign))
+
+    def t_main(sign, s):
+        i = (sign + 1) // 2
+        source = tm_out.at[i, s] if s else t_block(z + span_z)
+        return remote(source, tm_in.at[i, s], tm_s.at[i, s], tm_r.at[i, s], at_z(z + 2 * sign))
+
+    def t_gather(sign, j, s):
+        t_odd(sign, j).wait_recv()
+        found = to_in[(sign + 1) // 2, j].astype(F32)
+        if s > (sign < 0):
+            t_main(sign, s - 1).wait_recv()
+            found += tm_in[(sign + 1) // 2, s - 1].astype(F32)
+        return found
+
+    def t_step(s):
+        if s >= span_z // 2:
+            return
+        for sign in (-1, 1):
+            j = span_z // 2 - s
+            found = t_gather(sign, j, s) + t_block(z + sign * 2 * j)[...].astype(F32)
+            tm_out[(sign + 1) // 2, s] = found.astype(BF16)
+            t_main(sign, s).start()
+
+    t_sent = [t_main(1, 0)] + [t_odd(sign, j) for j in range(span_z // 2 - 1, -1, -1) for sign in (-1, 1)]
+
+    def t_over_x(d):
         q = lax.rem(x + d, nx)
-        return remote(
-            t_own.at[half, rows_of(q, xrows), :], tx_in.at[d - 1, half], tx_s.at[half, d - 1], tx_r.at[half, d - 1], at_x(q)
-        )
+        return remote(t_rows.at[q], tx_in.at[x], tx_s.at[d - 1], tx_r.at[d - 1], at_x(q))
 
     for i in range(groups):
         take_group(in_turn(i))
@@ -202,6 +237,9 @@
         def _(r):
             span = rows_of(r, step)
             t_own[half, span, :] = (t_own[half, span, :].astype(F32) + t_in[half, span, :].astype(F32)).astype(BF16)
+
+    for copy in t_sent:
+        copy.start()
 
     for i in range(per_half):
         pass_to_core(in_turn(i))
@@ -231,10 +269,7 @@
 
     for i in range(per_half, groups):
         pass_to_core(in_turn(i))
-
-    for half in range(2):
-        for d in range(1, nx):
-            t_over_x(half, d).start()
+    t_step(1)
 
     far = 1 - zhi
     arrived(far)
@@ -289,6 +324,7 @@
             to_core(half, pair).start()
 
     for_partner(0)
+    t_step(2)
     stats_cx(1).wait()
     mine = s_cx[here, 0:1, :]
     theirs = s_cx[x * 2 + other, 0:1, :]
@@ -326,6 +362,12 @@
         for_self(0, pair)
 
     for_partner(1)
+
+    @pl.loop(0, pairs)
+    def _(pair):
+        for_self(1, pair)
+
+    t_step(3)
 
     for n in range(2, 2 * nx):
         stats_cx(n).wait()
@@ -348,14 +390,12 @@
         stats_z(d).start()
 
     flat[...] = jnp.transpose(srow[:, own_lanes], (1, 0))
-    own_rows = rows_of(x, xrows)
-
-    @pl.loop(0, pairs)
-    def _(pair):
-        for_self(1, pair)
-
-    @pl.loop(0, 2)
-    def _(half):
+
+
+    def to_z(k):
+        return remote(z_out.at[k], z_in.at[z], rz_s.at[k], rz_r.at[z], at_z(k))
+
+    def z_half(half):
         for d in range(1, nx):
             for pair in range(pairs):
                 to_x(half, pair, d).wait_recv()
@@ -363,30 +403,6 @@
         for d in range(1, nx):
             whole += x_in[d - 1, half].astype(F32) * flat[0:xrows, 4 + d : 5 + d]
         acc[half] = whole
-
-    @pl.loop(1, nz)
-    def _(d):
-        stats_z(d).wait()
-
-    top, summed, label = joined(s_z[...])
-    srow[0:1, 0:LANES] = jnp.exp(s_z[z, 0:1, :] - top) / summed
-    flat[...] = jnp.transpose(srow[:, 0:LANES], (1, 0))
-    s_loss[x] = jnp.broadcast_to(jnp.log(summed) + top - label, (8, LANES))
-
-    def losses(d):
-        return remote(s_loss.at[x], s_loss.at[x], sl_s.at[d - 1], sl_r.at[d - 1], at_x(x + d))
-
-    def to_z(k):
-        return remote(z_out.at[k], z_in.at[z], rz_s.at[k], rz_r.at[z], at_z(k))
-
-    @pl.loop(0, 2)
-    def _(half):
-        weight = tcol[own_rows, 1:2]
-        hit = t_own[half, own_rows, :].astype(F32)
-        for d in range(1, nx):
-            t_over_x(half, d).wait_recv()
-            hit += tx_in[d - 1, half].astype(F32)
-        acc[half] = acc[half] * (weight * flat[0:xrows, 0:1]) - weight * hit
         for low in range(nzlo):
             slot = low % 4
             for j in range(quarters):
@@ -397,12 +413,43 @@
             def _():
                 tall[4] = tall[slot]
 
-            z_out[k] = tall[slot].astype(BF16)
-
-    to_z(lax.rem(z + nz // 2, nz)).start()
-    for d in range(nz // 2 - 1, 0, -1):
-        to_z(lax.rem(z + d, nz)).start()
-        to_z(lax.rem(z + nz - d, nz)).start()
+            @pl.when(k != z)
+            def _():
+                z_out[k] = tall[slot].astype(BF16)
+                to_z(k).start()
+
+    z_half(0)
+    z_half(1)
+    whole = t_block(z)[...].astype(F32)
+    for sign in (-1, 1):
+        whole += t_gather(sign, 0, span_z // 2)
+    t_wide[...] = whole
+    for i in range(nx):
+        t_rows[i] = t_wide[i * rb : (i + 1) * rb, :].astype(BF16)
+    for d in range(1, nx):
+        t_over_x(d).start()
+    tx_in[x] = t_rows[x]
+
+    @pl.loop(1, nz)
+    def _(d):
+        stats_z(d).wait()
+
+    top, summed, label = joined(s_z[...])
+    for d in range(nz):
+        srow[d : d + 1, 0:LANES] = jnp.exp(s_z[lax.rem(z + nz - d, nz), 0:1, :] - top) / summed
+    flat[...] = jnp.transpose(srow[:, 0:LANES], (1, 0))
+    for low in range(nzlo):
+
+        @pl.when(zlo == low)
+        def _():
+            for j in range(quarters):
+                tall_col[0, j * rb : (j + 1) * rb, :] = flat[low * rb : (low + 1) * rb, :]
+                tall_col[1, j * rb : (j + 1) * rb, :] = own_col[low * rb : (low + 1) * rb, :]
+
+    s_loss[x] = jnp.broadcast_to(jnp.log(summed) + top - label, (8, LANES))
+
+    def losses(d):
+        return remote(s_loss.at[x], s_loss.at[x], sl_s.at[d - 1], sl_r.at[d - 1], at_x(x + d))
 
     for d in range(1, nx):
         losses(d).start()
@@ -417,15 +464,21 @@
             logits[to : to + rb, 0:LANES] = stat[of : of + rb, :]
     loss_ref[...] = jnp.transpose(logits[:, 0:LANES], (1, 0))[0:1, :].reshape(rows)
 
-    @pl.loop(0, nz)
-    def _(k):
-        @pl.when(k != z)
-        def _():
-            remote(z_in.at[k], z_in.at[k], rz_s.at[k], rz_r.at[k], at_core).wait_recv()
-            tall[4] += z_in[k].astype(F32)
-
+    for d in range(1, nx):
+        t_over_x(d).wait_recv()
+    hit = tx_in[0].astype(F32)
+    for i in range(1, nx):
+        hit += tx_in[i].astype(F32)
+    total = tall[4] * tall_col[0, :, 0:1]
+    for d in range(1, nz):
+        k = lax.rem(z + nz - d, nz)
+        remote(z_in.at[k], z_in.at[k], rz_s.at[k], rz_r.at[k], at_core).wait_recv()
+        total += z_in[k].astype(F32) * tall_col[0, :, d : d + 1]
+    tall[4] = total
     for j in range(quarters):
-        out_ref[:, j * LANES : (j + 1) * LANES] = tall[4, j * rb : (j + 1) * rb, :].astype(BF16)
+        lanes = slice(j * LANES, (j + 1) * LANES)
+        soft_part = tall[4, j * rb : (j + 1) * rb, :]
+        out_ref[:, lanes] = (tall_col[1, 0:rb, 1:2] * (soft_part - hit[:, lanes])).astype(BF16)
 
     @pl.loop(1, nz)
     def _(d):
@@ -433,6 +486,10 @@
 
     for copy in direct + onward + backward:
         copy.wait_send()
+    for copy in t_sent + [t_main(sign, s) for s in range(1, span_z // 2) for sign in (-1, 1)]:
+        copy.wait_send()
+    for d in range(1, nx):
+        t_over_x(d).wait_send()
 
     @pl.loop(0, groups)
     def _(g):
@@ -444,8 +501,6 @@
     @pl.loop(0, 2)
     def _(half):
         t_core(half).wait_send()
-        for d in range(1, nx):
-            t_over_x(half, d).wait_send()
         for pair in range(pairs):
             to_core(half, pair).wait_send()
             for d in range(1, nx):
@@ -462,9 +517,11 @@
     size = min(4, nzlo)
     groups = nz // size
     tallness = rb * wide // LANES
+    zrows, reach = nx * rb, nz // 4
     pairs = wide // TILE
     vmem, dma = pltpu.VMEM, pltpu.SemaphoreType.DMA
     spec = pl.BlockSpec(memory_space=pltpu.VMEM)
+    chain = vmem((2, reach, zrows, wide), BF16)
     halves = vmem((2, rows, wide), BF16)
     scratch = [
         vmem((rb, wide), BF16), vmem((rows,), jnp.int32), vmem((rows,), F32), dma((3,)),
@@ -476,13 +533,15 @@
         vmem((nx * LANES, LANES), F32), vmem((LANES, nx * LANES), F32),
         vmem((2 * nx, 4, nx * LANES), F32), vmem((nz, 4, LANES), F32), vmem((nx, 8, LANES), F32),
         dma((2 * nx,)), dma((2 * nx,)), dma((nz,)), dma((nz,)), dma((nx - 1,)), dma((nx - 1,)),
-        halves, halves, halves, vmem((nx - 1, 2, xrows, wide), BF16),
-        dma((2,)), dma((2,)), dma((2, nx - 1)), dma((2, nx - 1)),
+        halves, halves, halves, dma((2,)), dma((2,)),
+        chain, chain, chain, dma((2, reach)), dma((2, reach)), dma((2, reach)), dma((2, reach)),
+        vmem((nx, rb, wide), BF16), vmem((nx, rb, wide), BF16), dma((nx - 1,)), dma((nx - 1,)),
         halves, halves, dma((2 * pairs,)), dma((2 * pairs,)), vmem((rows, TILE), F32),
         halves, vmem((nx - 1, 2, xrows, wide), BF16), vmem((2, xrows, wide), F32),
-        dma((2 * pairs, nx - 1)), dma((2 * pairs, nx - 1)),
+        dma((2 * pairs, nx - 1)), dma((2 * pairs, nx - 1)), vmem((zrows, wide), F32),
         vmem((2, xrows, wide), F32), vmem((nz, tallness, LANES), BF16), vmem((nz, tallness, LANES), BF16),
         dma((nz,)), dma((nz,)), vmem((LANES, LANES), F32), vmem((2, rows, LANES), F32),
+        vmem((xrows, LANES), F32), vmem((2, tallness, LANES), F32),
     ]
     return pl.pallas_call(
         functools.partial(kernel, dims),

time: 65.1 us -> 61.4 us (0.943); the launches traced: 64.9 us -> 60.2 us
  Pallas kernels: 63.1 us -> 58.4 us
    pallas_call x1, Pallas kernels: 63.1 us -> 58.4 us  [per_device(): pl.pallas_call(functools.partial(kernel, dims), out_shape=(pltpu.VMEM((rb...]
where the time goes in v6:
time: 61.4 us; the launch traced here: 60.2 us
  Pallas kernels  58.4 us (95%)
  local copies, waits for them, and re-layouts  1.19 us (2%)
  between operations  0.64 us (1%)
    pallas_call x1, Pallas kernels, per_device(): pl.pallas_call(functools.partial(kernel, dims), out_shape=(pltpu.VMEM((rb...  58.4 us

profile of v6, /device:TPU:24, one launch (start us, length us, event | category | flops | bytes accessed | tf_op | source)
XLA Modules:
  0.0 60.2 jit_solution(6398848109804868342)
XLA Ops:
  0.6 58.4 %shard_map.59 = (bf16[12,512]{1,0:T(8,128)(2,1)S(1)}, f32[384]{0:T(512)S(1)}) custom-call(bf16[12,512]{1,0:T(8,128)(2,1)} %h_hbm.1, bf16[2048,1152]{1,0:T(8,128)(2,1)} %w_hbm.1, s32[384]{0:T(512)} %t_hbm.1, f32[384]{0:T(512)} %rw_hbm.1), custom_call_target="tpu_custom_call" | custom-call | tf_op jit(solution)/shard_map/pallas_call | solution.py:546
  59.0 0.6 %copy.8 = bf16[12,512]{1,0:T(8,128)(2,1)} copy(bf16[12,512]{1,0:T(8,128)(2,1)S(1)} %get-tuple-element.2) | data formatting | bytes 24576
  59.6 0.6 copy.9

commit v7 on v6

--- a/solution.py
+++ b/solution.py
@@ -22,7 +22,7 @@
     logits, soft, tcol, stat, srow, s_cx, s_z, s_loss, sc_s, sc_r, sz_s, sz_r, sl_s, sl_r,
     t_out, t_in, t_own, tc_s, tc_r, to_in, tm_in, tm_out, to_s, to_r, tm_s, tm_r, t_rows, tx_in, tx_s, tx_r,
     c_out, c_in, rc_s, rc_r, whole_ref, x_out, x_in, x_own, rx_s, rx_r, t_wide,
-    acc, z_out, z_in, rz_s, rz_r, flat, factor, own_col, tall_col,
+    acc, z_out, z_in, rz_s, rz_r, flat, factor, own_col, tall_col, spread,
 ):
     nzlo, nx = dims
     nz = 2 * nzlo
@@ -409,14 +409,19 @@
                 tall[slot, j * rb : (j + 1) * rb, :] = acc[half, low * rb : (low + 1) * rb, j * LANES : (j + 1) * LANES]
             k = half * nzlo + low
 
+            z_out[k] = tall[slot].astype(BF16)
+
             @pl.when(k == z)
             def _():
                 tall[4] = tall[slot]
 
-            @pl.when(k != z)
-            def _():
-                z_out[k] = tall[slot].astype(BF16)
-                to_z(k).start()
+        for d in range(nz // 2, 0, -1):
+            for sign in (1, -1)[: 1 + (d < nz // 2)]:
+                to = lax.rem(z + sign * d + nz, nz)
+
+                @pl.when(to // nzlo == half)
+                def _():
+                    to_z(to).start()
 
     z_half(0)
     z_half(1)
@@ -453,6 +458,8 @@
 
     for d in range(1, nx):
         losses(d).start()
+    for d in range(nz):
+        spread[d] = jnp.broadcast_to(tall_col[0, :, d : d + 1], spread.shape[1:])
     for d in range(1, nx):
         losses(d).wait()
     for i in range(nx):
@@ -469,11 +476,11 @@
     hit = tx_in[0].astype(F32)
     for i in range(1, nx):
         hit += tx_in[i].astype(F32)
-    total = tall[4] * tall_col[0, :, 0:1]
+    total = tall[4] * spread[0]
     for d in range(1, nz):
         k = lax.rem(z + nz - d, nz)
         remote(z_in.at[k], z_in.at[k], rz_s.at[k], rz_r.at[k], at_core).wait_recv()
-        total += z_in[k].astype(F32) * tall_col[0, :, d : d + 1]
+        total += z_in[k].astype(F32) * spread[d]
     tall[4] = total
     for j in range(quarters):
         lanes = slice(j * LANES, (j + 1) * LANES)
@@ -505,6 +512,17 @@
             to_core(half, pair).wait_send()
             for d in range(1, nx):
                 to_x(half, pair, d).wait_send()
+
+
+def finish(grad, loss, grad_out, loss_out, sem):
+    copies = [
+        pltpu.make_async_copy(grad, grad_out, sem.at[0]),
+        pltpu.make_async_copy(loss, loss_out, sem.at[1]),
+    ]
+    for copy in copies:
+        copy.start()
+    for copy in copies:
+        copy.wait()
 
 
 def per_device(dims, hidden, weight, targets, row_weight):
@@ -541,9 +559,9 @@
         dma((2 * pairs, nx - 1)), dma((2 * pairs, nx - 1)), vmem((zrows, wide), F32),
         vmem((2, xrows, wide), F32), vmem((nz, tallness, LANES), BF16), vmem((nz, tallness, LANES), BF16),
         dma((nz,)), dma((nz,)), vmem((LANES, LANES), F32), vmem((2, rows, LANES), F32),
-        vmem((xrows, LANES), F32), vmem((2, tallness, LANES), F32),
+        vmem((xrows, LANES), F32), vmem((2, tallness, LANES), F32), vmem((nz, tallness, LANES), F32),
     ]
-    return pl.pallas_call(
+    results = pl.pallas_call(
         functools.partial(kernel, dims),
         out_shape=(
             pltpu.VMEM((rb, wide), BF16),
@@ -554,6 +572,17 @@
         scratch_shapes=scratch,
         compiler_params=pltpu.CompilerParams(collective_id=0, has_side_effects=True),
     )(hidden, weight, targets, row_weight)
+    anywhere = pl.BlockSpec(memory_space=pl.ANY)
+    return pl.pallas_call(
+        finish,
+        out_shape=(
+            jax.ShapeDtypeStruct((rb, wide), BF16),
+            jax.ShapeDtypeStruct((rows,), F32),
+        ),
+        in_specs=[anywhere, anywhere],
+        out_specs=(anywhere, anywhere),
+        scratch_shapes=[dma((2,))],
+    )(*(pltpu.with_memory_space_constraint(result, pltpu.VMEM) for result in results))
 
 
 def on_mesh(split):

time: 61.4 us -> 60.5 us (0.985)
  local copies, waits for them, and re-layouts: 1.19 us -> 0 us
  Pallas kernels: 58.4 us -> 59.1 us
    unnamed x2 -> x0, local copies, waits for them, and re-layouts: 1.19 us -> none
    pallas_call x0 -> x1, Pallas kernels: none -> 0.63 us  [per_device(): pl.pallas_call(finish, out_shape=(jax.ShapeDtypeStruct((rb, wide), BF16),...]
where the time goes in v7:
time: 60.5 us; the launch traced here: 59.7 us
  Pallas kernels  59.1 us (98%)
  between operations  0.64 us (1%)
    pallas_call x1, Pallas kernels, per_device(): pl.pallas_call(functools.partial(kernel, dims), out_shape=(pltpu.VMEM((rb...  58.5 us

profile of v7, /device:TPU:24, one launch (start us, length us, event | category | flops | bytes accessed | tf_op | source)
XLA Modules:
  0.0 59.7 jit_solution(3294960771955471405)
XLA Ops:
  0.6 58.5 %shard_map.59 = (bf16[12,512]{1,0:T(8,128)(2,1)S(1)}, f32[384]{0:T(512)S(1)}) custom-call(bf16[12,512]{1,0:T(8,128)(2,1)} %h_hbm.1, bf16[2048,1152]{1,0:T(8,128)(2,1)} %w_hbm.1, s32[384]{0:T(512)} %t_hbm.1, f32[384]{0:T(512)} %rw_hbm.1), custom_call_target="tpu_custom_call" | custom-call | tf_op jit(solution)/shard_map/pallas_call | solution.py:564
  59.1 0.6 %shard_map.60 = (bf16[12,512]{1,0:T(8,128)(2,1)}, f32[384]{0:T(512)}) custom-call(bf16[12,512]{1,0:T(8,128)(2,1)S(1)} %get-tuple-element.4.grad, f32[384]{0:T(512)S(1)} %get-tuple-element.5.loss), custom_call_target="tpu_custom_call" | custom-call | tf_op jit(solution)/shard_map/pallas_call | solution.py:576

commit v8 on v7

--- a/solution.py
+++ b/solution.py
@@ -30,7 +30,7 @@
     quarters = wide // LANES
     rows = nzlo * nx * rb
     xrows = nzlo * rb
-    step = 48
+    step, few = 48, 16
     vocab = w_ref.shape[1]
     per_x = xrows // step
     zlo, x = lax.axis_index("zlo"), lax.axis_index("x")
@@ -102,8 +102,8 @@
     own_col[...] = tcol[own_rows, :]
 
     offset = ((zlo * nx + x) * 4 + zhi * 2 + core) * vocab
-    lane = lax.broadcasted_iota(jnp.int32, (step, LANES), 1)
-    column = lax.broadcasted_iota(jnp.int32, (step, vocab), 1)
+    lane = lax.broadcasted_iota(jnp.int32, (few, LANES), 1)
+    column = lax.broadcasted_iota(jnp.int32, (few, vocab), 1)
 
     def is_target(span, of=tcol):
         wanted = of[span, 0:1].astype(jnp.int32) - offset
@@ -111,8 +111,9 @@
 
     @pl.loop(0, rows // step)
     def _(r):
-        span = rows_of(r, step)
-        soft[span, :] = jnp.where(is_target(span, stat), 1.0, 0.0).astype(BF16)
+        for i in range(step // few):
+            span = pl.ds(pl.multiple_of(r * step + i * few, few), few)
+            soft[span, :] = jnp.where(is_target(span, stat), 1.0, 0.0).astype(BF16)
 
     def product(half, who, pair):
         first = (half * 2 + who) * wide + pair * TILE
@@ -122,9 +123,9 @@
     def tile(pair):
         return rows_of(pair, TILE)
 
-    def padded(r):
-        first = (r // per_x) * LANES + lax.rem(r, per_x) * step
-        return pl.ds(pl.multiple_of(first, 16), step)
+    def padded(r, more, size):
+        first = (r // per_x) * LANES + lax.rem(r, per_x) * step + more
+        return pl.ds(pl.multiple_of(first, 16), size)
 
     w_copy.wait()
 
@@ -284,14 +285,17 @@
 
     @pl.loop(0, rows // step)
     def _(r):
-        span = rows_of(r, step)
-        part = logits[span, :]
-        top = jnp.max(part, axis=1, keepdims=True)
-        shifted = jnp.exp(part - top)
-        soft[span, :] = shifted.astype(BF16)
-        summed = jnp.sum(shifted, axis=1, keepdims=True)
-        label = jnp.sum(jnp.where(is_target(span), part, 0.0), axis=1, keepdims=True)
-        stat[padded(r), :] = jnp.where(lane == 0, top, jnp.where(lane == 1, summed, jnp.where(lane == 2, label, 0.0)))
+        for i in range(step // few):
+            span = pl.ds(pl.multiple_of(r * step + i * few, few), few)
+            part = logits[span, :]
+            top = jnp.max(part, axis=1, keepdims=True)
+            shifted = jnp.exp(part - top)
+            soft[span, :] = shifted.astype(BF16)
+            summed = jnp.sum(shifted, axis=1, keepdims=True)
+            label = jnp.sum(jnp.where(is_target(span), part, 0.0), axis=1, keepdims=True)
+            stat[padded(r, i * few, few), :] = jnp.where(
+                lane == 0, top, jnp.where(lane == 1, summed, jnp.where(lane == 2, label, 0.0))
+            )
 
     def joined(slots):
         tops = slots[:, 0:1, :]
@@ -354,7 +358,7 @@
             x_out[half, :, lanes] = whole.astype(BF16)
 
         x_own[half, :, tile(pair)] = whole_ref[rows_of(x, xrows), :]
-        for d in range(1, nx):
+        for d in sorted(range(1, nx), key=lambda d: -min(d, nx - d)):
             to_x(half, pair, d).start()
 
     @pl.loop(0, pairs)
@@ -460,6 +464,26 @@
         losses(d).start()
     for d in range(nz):
         spread[d] = jnp.broadcast_to(tall_col[0, :, d : d + 1], spread.shape[1:])
+    for copy in direct + onward + backward:
+        copy.wait_send()
+    for copy in t_sent + [t_main(sign, s) for s in range(1, span_z // 2) for sign in (-1, 1)]:
+        copy.wait_send()
+
+    @pl.loop(0, groups)
+    def _(g):
+        over_core(g, 0).wait_send()
+        for d in range(1, nx):
+            over_core(g, d).wait_send()
+            over_x(g, d).wait_send()
+
+    @pl.loop(0, 2)
+    def _(half):
+        t_core(half).wait_send()
+        for pair in range(pairs):
+            to_core(half, pair).wait_send()
+            for d in range(1, nx):
+                to_x(half, pair, d).wait_send()
+
     for d in range(1, nx):
         losses(d).wait()
     for i in range(nx):
@@ -487,31 +511,12 @@
         soft_part = tall[4, j * rb : (j + 1) * rb, :]
         out_ref[:, lanes] = (tall_col[1, 0:rb, 1:2] * (soft_part - hit[:, lanes])).astype(BF16)
 
+    for d in range(1, nx):
+        t_over_x(d).wait_send()
+
     @pl.loop(1, nz)
     def _(d):
         to_z(lax.rem(z + d, nz)).wait_send()
-
-    for copy in direct + onward + backward:
-        copy.wait_send()
-    for copy in t_sent + [t_main(sign, s) for s in range(1, span_z // 2) for sign in (-1, 1)]:
-        copy.wait_send()
-    for d in range(1, nx):
-        t_over_x(d).wait_send()
-
-    @pl.loop(0, groups)
-    def _(g):
-        over_core(g, 0).wait_send()
-        for d in range(1, nx):
-            over_core(g, d).wait_send()
-            over_x(g, d).wait_send()
-
-    @pl.loop(0, 2)
-    def _(half):
-        t_core(half).wait_send()
-        for pair in range(pairs):
-            to_core(half, pair).wait_send()
-            for d in range(1, nx):
-                to_x(half, pair, d).wait_send()
 
 
 def finish(grad, loss, grad_out, loss_out, sem):

time: 60.5 us -> 60 us (level)
  the two profiles are of different devices: /device:TPU:24 before, /device:TPU:40 now
where the time goes in v8:
time: 60 us; the launch traced here: 59.8 us
  Pallas kernels  59.1 us (98%)
  between operations  0.64 us (1%)
    pallas_call x1, Pallas kernels, per_device(): pl.pallas_call(functools.partial(kernel, dims), out_shape=(pltpu.VMEM((rb...  58.5 us

profile of v8, /device:TPU:40, one launch (start us, length us, event | category | flops | bytes accessed | tf_op | source)
XLA Modules:
  0.0 59.8 jit_solution(18109988484706822867)
XLA Ops:
  0.6 58.5 %shard_map.59 = (bf16[12,512]{1,0:T(8,128)(2,1)S(1)}, f32[384]{0:T(512)S(1)}) custom-call(bf16[12,512]{1,0:T(8,128)(2,1)} %h_hbm.1, bf16[2048,1152]{1,0:T(8,128)(2,1)} %w_hbm.1, s32[384]{0:T(512)} %t_hbm.1, f32[384]{0:T(512)} %rw_hbm.1), custom_call_target="tpu_custom_call" | custom-call | tf_op jit(solution)/shard_map/pallas_call | solution.py:569
  59.2 0.6 %shard_map.60 = (bf16[12,512]{1,0:T(8,128)(2,1)}, f32[384]{0:T(512)}) custom-call(bf16[12,512]{1,0:T(8,128)(2,1)S(1)} %get-tuple-element.4.grad, f32[384]{0:T(512)S(1)} %get-tuple-element.5.loss), custom_call_target="tpu_custom_call" | custom-call | tf_op jit(solution)/shard_map/pallas_call | solution.py:581

commit v9 on v8

--- a/solution.py
+++ b/solution.py
@@ -371,8 +371,6 @@
     def _(pair):
         for_self(1, pair)
 
-    t_step(3)
-
     for n in range(2, 2 * nx):
         stats_cx(n).wait()
     all_top, all_sum, all_label = joined(s_cx[...])
@@ -392,6 +390,8 @@
     @pl.loop(1, nz)
     def _(d):
         stats_z(d).start()
+
+    t_step(3)
 
     flat[...] = jnp.transpose(srow[:, own_lanes], (1, 0))
 

time: 60 us -> 59.5 us (level)
  the two profiles are of different devices: /device:TPU:40 before, /device:TPU:24 now
where the time goes in v9:
time: 59.5 us; the launch traced here: 58.7 us
  Pallas kernels  58.1 us (98%)
  between operations  0.64 us (1%)
    pallas_call x1, Pallas kernels, per_device(): pl.pallas_call(functools.partial(kernel, dims), out_shape=(pltpu.VMEM((rb...  57.4 us

profile of v9, /device:TPU:24, one launch (start us, length us, event | category | flops | bytes accessed | tf_op | source)
XLA Modules:
  0.0 58.7 jit_solution(11001608680558750385)
XLA Ops:
  0.6 57.4 %shard_map.59 = (bf16[12,512]{1,0:T(8,128)(2,1)S(1)}, f32[384]{0:T(512)S(1)}) custom-call(bf16[12,512]{1,0:T(8,128)(2,1)} %h_hbm.1, bf16[2048,1152]{1,0:T(8,128)(2,1)} %w_hbm.1, s32[384]{0:T(512)} %t_hbm.1, f32[384]{0:T(512)} %rw_hbm.1), custom_call_target="tpu_custom_call" | custom-call | tf_op jit(solution)/shard_map/pallas_call | solution.py:569
  58.1 0.6 %shard_map.60 = (bf16[12,512]{1,0:T(8,128)(2,1)}, f32[384]{0:T(512)}) custom-call(bf16[12,512]{1,0:T(8,128)(2,1)S(1)} %get-tuple-element.4.grad, f32[384]{0:T(512)S(1)} %get-tuple-element.5.loss), custom_call_target="tpu_custom_call" | custom-call | tf_op jit(solution)/shard_map/pallas_call | solution.py:581
